TPU v7x, 32 devices: a whole 2x2x4 slice. The times are simulated.
32 devices in a mesh: row: 8 (over y, x, core), col: 4 (over z).
Axes of the slice: x: 2, y: 2, z: 4, core: 2. Of those that a mesh axis runs over, the one named last changes fastest.
Arguments:
- node_features: bfloat16 [8192, 128], P(('row', 'col')), may hold values from -6 to 6
- tile_values: bfloat16 [8, 4, 384, 128, 128], P('row', 'col'), may hold values from -0.078125 to 0.078125
- tile_rows: int32 [8, 4, 384], P('row', 'col'), may hold values from 0 to 7
- tile_cols: int32 [8, 4, 384], P('row', 'col'), may hold values from 0 to 15
- tile_count: int32 [8, 4], P('row', 'col'), may hold values from 48 to 384, as said below
- labels: int32 [8192], P(('row', 'col')), may hold values from 0 to 46
- train_mask: int32 [8192], P(('row', 'col')), may hold values from 0 to 1, as said below
- hidden_weight: bfloat16 [128, 256], replicated, may hold values from -0.5 to 0.5
- hidden_bias: float32 [256], replicated, may hold values from -3 to 3
- class_weight: bfloat16 [256, 47], replicated, may hold values from -3.59375 to 3.59375
- class_bias: float32 [47], replicated, may hold values from -4 to 4
Outputs:
- hidden: bfloat16 [8192, 256], P(('row', 'col'))
- logits: float32 [47, 8192], P(None, ('row', 'col'))
- mean_loss: float32 [], replicated
- hidden_weight_grad: float32 [128, 256], replicated
- hidden_bias_grad: float32 [256], replicated
- class_weight_grad: float32 [256, 47], replicated
- class_bias_grad: float32 [47], replicated
Inputs may be any that keep to these rules, and one draw needn't show every extreme that they name: Slots s >= tile_count of a block are not part of it; some block has all 384 slots live. `train_mask`: at least one node is a training node.
All inputs are finite; a program needn't handle non-finite values.
Results may differ from a plain program's by a relative error of at most 0.025.
Values may be sent and summed in bfloat16 or wider, within the bound.
No kernel may reach another device: no remote copies, remote signals or barrier semaphores. Data moves between devices by JAX's collectives and lax.ppermute only.
A program may use at most 128 MiB of HBM per device.

v0:
```python
import functools
import math

import jax
import jax.numpy as jnp
from jax import lax
from jax.experimental import pallas as pl
from jax.experimental.pallas import tpu as pltpu
from jax.sharding import PartitionSpec as P


TILE = 128
MASK_CODE = 128
MIB = 1024 * 1024
WIRE = jnp.bfloat16
f32 = jnp.float32
bf16 = jnp.bfloat16


VMEM = pl.BlockSpec(memory_space=pltpu.VMEM)
SMEM = pl.BlockSpec(memory_space=pltpu.SMEM)
HBM = pl.BlockSpec(memory_space=pltpu.HBM)


def params(limit):
    return pltpu.CompilerParams(vmem_limit_bytes=limit)


def cost(flops, moved, transcendentals=0):
    return pl.CostEstimate(flops=flops, bytes_accessed=moved, transcendentals=transcendentals)


def dot(a, b, dims=((1,), (0,))):
    return lax.dot_general(a, b, (dims, ((), ())), preferred_element_type=f32)


def halves(value):
    high = value.astype(bf16)
    return high, (value - high.astype(f32)).astype(bf16)


def collect_kernel(group, depth, tile_cols, count, rows_hbm, cols_hbm, values, total, ring, rows, cols, sem, table_sem):
    slots = values.shape[0]
    groups = slots // group
    spare = total.shape[0] - 1
    tables = [
        pltpu.make_async_copy(source, target, table_sem.at[k])
        for k, (source, target) in enumerate(((rows_hbm, rows), (cols_hbm, cols)))
    ]
    for table in tables:
        table.start()

    def copy(index, slot):
        return pltpu.make_async_copy(
            values.at[pl.ds(index * group, group)], ring.at[slot], sem.at[slot]
        )

    live = count[0, 0]
    groups_live = (live + group - 1) // group
    for slot in range(depth):
        @pl.when(slot < groups_live)
        def _():
            copy(slot, slot).start()

    @pl.loop(0, spare // 4)
    def _(place):
        for k in range(4):
            total[place * 4 + k] = jnp.zeros((TILE, TILE), f32)

    for table in tables:
        table.wait()

    @pl.loop(0, groups_live)
    def _(index):
        slot = lax.rem(index, depth)
        copy(index, slot).wait()
        for k in range(group):
            item = index * group + k
            place = rows[0, item] * tile_cols + cols[0, item]
            place = jnp.where(item < live, place, spare)
            total[place] = total[place] + ring[slot, k].astype(f32)

        if depth < groups:
            @pl.when(index + depth < groups_live)
            def _():
                copy(index + depth, slot).start()


def collect(values, rows, cols, count, tile_rows, tile_cols):
    slots = values.shape[0]
    n_places = tile_rows * tile_cols
    group = math.gcd(slots, 16)
    small = n_places <= 128
    depth = slots // group if small else min(slots // group, 8)
    rows, cols = (pltpu.with_memory_space_constraint(x, pltpu.HBM) for x in (rows, cols))
    return pl.pallas_call(
        functools.partial(collect_kernel, group, depth, tile_cols),
        out_shape=jax.ShapeDtypeStruct((n_places + 1, TILE, TILE), f32),
        in_specs=[SMEM, HBM, HBM, HBM],
        out_specs=VMEM,
        scratch_shapes=[
            pltpu.VMEM((depth, group, TILE, TILE), bf16),
            pltpu.SMEM((1, slots), jnp.int32),
            pltpu.SMEM((1, slots), jnp.int32),
            pltpu.SemaphoreType.DMA((depth,)),
            pltpu.SemaphoreType.DMA((2,)),
        ],
        compiler_params=params((44 if small else 56) * MIB),
        cost_estimate=cost(slots * TILE * TILE, slots * TILE * TILE * 2),
        name="collect",
    )(count, rows, cols, values)


def position(row, k, n_row):
    other = row ^ k
    return (other & 1) * (n_row // 2) + (other >> 1)


def place_of(row, k, n_row, nodes):
    return pl.ds(pl.multiple_of(position(row, k, n_row) * nodes, nodes), nodes)


def stack(row, start, pieces, stacked):
    nodes = pieces[0].shape[0]
    for k, piece in enumerate(pieces):
        place = pl.multiple_of(((row ^ (start + 2 * k)) >> 1) * nodes, nodes)
        stacked[pl.ds(place, nodes), :] = piece[...]


def parity_columns(parity, columns):
    return pl.ds(pl.multiple_of(parity * (columns // 2), columns // 2), columns // 2)


def first_near_kernel(n_row, ids, total, *refs):
    pieces = refs[: n_row // 2]
    dense, part, stacked = refs[n_row // 2 :]
    row = ids[0]
    stack(row, 0, pieces, stacked)
    tile_rows = dense.shape[0] // TILE
    tile_cols = dense.shape[1] // TILE
    each = tile_cols // n_row

    @pl.loop(0, tile_rows)
    def _(tile_row):
        lines = pl.ds(pl.multiple_of(tile_row * TILE, TILE), TILE)
        for tile_col in range(tile_cols):
            target = position(tile_col // each, 0, n_row) * each + tile_col % each
            lanes = pl.ds(target * TILE, TILE)
            dense[lines, lanes] = total[tile_row * tile_cols + tile_col].astype(bf16)

    part[...] = dot(dense[:, parity_columns(row & 1, dense.shape[1])], stacked[...])


def first_near(ids, total, pieces, n_col):
    nodes, width = pieces[0].shape
    n_row = 2 * len(pieces)
    size = (n_col * nodes, n_row * nodes)
    return pl.pallas_call(
        functools.partial(first_near_kernel, n_row),
        out_shape=[jax.ShapeDtypeStruct(size, bf16), jax.ShapeDtypeStruct((size[0], width), f32)],
        in_specs=[SMEM, VMEM] + [VMEM] * len(pieces),
        out_specs=[VMEM] * 2,
        scratch_shapes=[pltpu.VMEM((len(pieces) * nodes, width), bf16)],
        compiler_params=params(size[0] * size[1] * 6 + 6 * MIB),
        cost_estimate=cost(size[0] * size[1] * width, size[0] * size[1] * 6),
        name="first_near",
    )(ids, total, *pieces)


def first_far_kernel(n_row, n_col, ids, dense, part, *refs):
    pieces = refs[: n_row // 2]
    outs, stacked = refs[n_row // 2 : -1], refs[-1]
    nodes = pieces[0].shape[0]
    row, col = ids[0], ids[1]
    stack(row, 1, pieces, stacked)
    columns = parity_columns(1 - (row & 1), dense.shape[1])
    for k in range(n_col):
        lines = pl.ds(pl.multiple_of((col ^ k) * nodes, nodes), nodes)
        outs[k][...] = (part[lines, :] + dot(dense[lines, columns], stacked[...])).astype(bf16)


def first_far(ids, dense, part, pieces, n_col):
    nodes, width = pieces[0].shape
    n_row = 2 * len(pieces)
    return pl.pallas_call(
        functools.partial(first_far_kernel, n_row, n_col),
        out_shape=[jax.ShapeDtypeStruct((nodes, width), bf16)] * n_col,
        in_specs=[SMEM, VMEM, VMEM] + [VMEM] * len(pieces),
        out_specs=[VMEM] * n_col,
        scratch_shapes=[pltpu.VMEM((len(pieces) * nodes, width), bf16)],
        compiler_params=params(dense.size * 2 + 6 * MIB),
        cost_estimate=cost(dense.size * width, dense.size),
        name="first_far",
    )(ids, dense, part, *pieces)


def hidden_kernel(n_row, n_col, ids, dense, weight, bias, class_weight, code, *refs):
    pieces = refs[:n_row]
    hidden_out, column_out, term_out, stacked = refs[n_row:]
    nodes = pieces[0].shape[0]
    row, col = ids[0], ids[1]
    for k in range(n_row):
        pre = dot(pieces[k][...], weight[...]) + bias[...]
        hidden = (pre * (1.0 / (1.0 + jnp.exp(-pre)))).astype(bf16)
        place = place_of(row, k, n_row, nodes)
        column_out[place, :] = hidden
        if k == 0:
            hidden_out[...] = hidden
        high, low = halves(dot(hidden, class_weight[...], ((1,), (1,))))
        stacked[place, :] = jnp.concatenate([high, low], axis=1)
    both = dot(dense[...], stacked[...])
    lanes = both.shape[1] // 2
    term = (both[:, :lanes] + both[:, lanes:]).T[: term_out.shape[0]]
    slice_of = lax.broadcasted_iota(jnp.int32, term.shape, 1) // nodes
    line = lax.broadcasted_iota(jnp.int32, term.shape, 0)
    codes = jnp.where(slice_of == col, jnp.concatenate([code[...]] * n_col, axis=1), 0.0)
    term_out[...] = jnp.where(line == term.shape[0] - 1, codes, term).astype(bf16)


def hidden_terms(ids, dense, weight, bias, class_weight, code, pieces, n_col, lines):
    nodes = pieces[0].shape[0]
    n_row = len(pieces)
    width = weight.shape[1]
    lanes = class_weight.shape[0]
    column = n_row * nodes
    return pl.pallas_call(
        functools.partial(hidden_kernel, n_row, n_col),
        out_shape=[
            jax.ShapeDtypeStruct((nodes, width), bf16),
            jax.ShapeDtypeStruct((column, width), bf16),
            jax.ShapeDtypeStruct((lines, n_col * nodes), bf16),
        ],
        in_specs=[SMEM] + [VMEM] * (5 + n_row),
        out_specs=[VMEM] * 3,
        scratch_shapes=[pltpu.VMEM((column, 2 * lanes), bf16)],
        compiler_params=params(dense.size * 2 + column * width * 8 + 6 * MIB),
        cost_estimate=cost(4 * dense.size * lanes, dense.size * 2, column * width * 2),
        name="hidden_terms",
    )(ids, dense, weight, bias, class_weight, code, *pieces)


def slope_kernel(n_row, ids, weight, bias, *refs):
    pieces = refs[:n_row]
    slope_out, turned_out = refs[n_row:]
    nodes = pieces[0].shape[0]
    row = ids[0]
    for k in range(n_row):
        pre = dot(pieces[k][...], weight[...]) + bias[...]
        sigma = 1.0 / (1.0 + jnp.exp(-pre))
        place = place_of(row, k, n_row, nodes)
        slope_out[place, :] = sigma * (1.0 + pre * (1.0 - sigma))
        turned_out[:, place] = pieces[k][...].T


def slopes(ids, weight, bias, pieces):
    nodes, features = pieces[0].shape
    n_row = len(pieces)
    width = weight.shape[1]
    column = n_row * nodes
    return pl.pallas_call(
        functools.partial(slope_kernel, n_row),
        out_shape=[
            jax.ShapeDtypeStruct((column, width), f32),
            jax.ShapeDtypeStruct((features, column), bf16),
        ],
        in_specs=[SMEM] + [VMEM] * (2 + n_row),
        out_specs=[VMEM] * 2,
        compiler_params=params(column * width * 8 + 4 * MIB),
        cost_estimate=cost(2 * column * features * width, column * width * 4, column * width * 2),
        name="slopes",
    )(ids, weight, bias, *pieces)


def tree_sum(parts):
    parts = [part.astype(f32) for part in parts]
    while len(parts) > 1:
        parts = [parts[k] + parts[k + 1] for k in range(0, len(parts), 2)]
    return parts[0]


def gradient_kernel(n_col, classes, ids, dense, column, slope, turned, class_weight_turned, class_bias, *refs):
    terms = refs[:n_col]
    logits_out, keep_out, send_out, scratch, packed = refs[n_col:]
    lines, nodes_row = terms[0].shape
    nodes = nodes_row // n_col
    features = turned.shape[0]
    width = column.shape[1]
    row, col = ids[0], ids[1]
    total = tree_sum([term[...] for term in terms])
    code = total[lines - 1 :, :]
    live = (code >= MASK_CODE).astype(f32)
    label = (code - MASK_CODE * live).astype(jnp.int32)
    line = lax.broadcasted_iota(jnp.int32, total.shape, 0)
    bias = jnp.broadcast_to(class_bias[...], (8, class_bias.shape[1])).T[:lines, :1]
    logits = jnp.where(line < classes, total + bias, -jnp.inf)
    scratch[...] = logits
    own = pl.ds(pl.multiple_of(col * nodes, nodes), nodes)
    logits_out[...] = scratch[:classes, own]
    top = jnp.max(logits, axis=0, keepdims=True)
    log_total = top + jnp.log(jnp.sum(jnp.exp(logits - top), axis=0, keepdims=True))
    chosen = line == label
    picked = jnp.sum(jnp.where(chosen, logits, 0.0), axis=0, keepdims=True)
    grad = (jnp.exp(logits - log_total) - chosen.astype(f32)) * live
    high, low = halves(grad)
    stacked = jnp.concatenate([high, low], axis=0)
    both = dot(stacked, dense[...])
    back = both[:lines] + both[lines:]
    back_high, back_low = halves(back)
    back_both = jnp.concatenate([back_high, back_low], axis=0)
    class_both = dot(back_both, column[...])
    packed[pl.ds(features, lines), :] = class_both[:lines] + class_both[lines:]
    twice = jnp.concatenate([class_weight_turned[:lines, :]] * 2, axis=0)
    hidden_grad = dot(back_both, twice, ((0,), (0,)))
    pre_grad = hidden_grad * slope[...]
    packed[pl.ds(0, features), :] = dot(turned[...], pre_grad.astype(bf16))
    packed[pl.ds(features + lines - 1, 1), :] = jnp.sum(pre_grad, axis=0, keepdims=True)
    here = (lax.broadcasted_iota(jnp.int32, (8, nodes_row), 1) // nodes == col).astype(f32)
    ours = here.astype(bf16)
    class_sum = dot(ours, high, ((1,), (1,))) + dot(ours, low, ((1,), (1,)))
    class_sum = jnp.concatenate([class_sum, jnp.zeros((8, width - lines), f32)], axis=1)
    loss = jnp.sum((log_total - picked) * live * here[:1])
    members = jnp.sum(live * here[:1])
    lane = lax.broadcasted_iota(jnp.int32, (8, width), 1)
    entry = lax.broadcasted_iota(jnp.int32, (8, width), 0)
    loss = jnp.full((8, width), loss, f32)
    loss_high = loss.astype(bf16).astype(f32)
    loss_middle = (loss - loss_high).astype(bf16).astype(f32)
    loss_low = loss - loss_high - loss_middle
    values = jnp.where(entry == 0, loss_high, jnp.where(entry == 1, loss_middle, loss_low))
    values = jnp.where(entry == 3, members, jnp.where(entry < 3, values, 0.0))
    tail = jnp.where(lane == row * n_col + col, values, 0.0)
    packed[pl.ds(features + lines, 8), :] = class_sum
    packed[pl.ds(features + lines + 8, 8), :] = tail
    part = packed.shape[0] // 2
    core = row & 1
    keep_out[...] = packed[pl.ds(pl.multiple_of(core * part, 8), part), :].astype(keep_out.dtype)
    send_out[...] = packed[pl.ds(pl.multiple_of((1 - core) * part, 8), part), :].astype(send_out.dtype)


def gradients(ids, dense, column, slope, turned, class_weight_turned, class_bias, terms, classes):
    n_col = len(terms)
    lines, nodes_row = terms[0].shape
    width = column.shape[1]
    packed = turned.shape[0] + lines + 16
    return pl.pallas_call(
        functools.partial(gradient_kernel, n_col, classes),
        out_shape=[
            jax.ShapeDtypeStruct((classes, nodes_row // n_col), f32),
            jax.ShapeDtypeStruct((packed // 2, width), WIRE),
            jax.ShapeDtypeStruct((packed // 2, width), WIRE),
        ],
        in_specs=[SMEM] + [VMEM] * (6 + n_col),
        out_specs=[VMEM] * 3,
        scratch_shapes=[
            pltpu.VMEM((lines, nodes_row), f32),
            pltpu.VMEM((packed, width), f32),
        ],
        compiler_params=params(dense.size * 2 + column.size * 16 + 6 * MIB),
        cost_estimate=cost(4 * dense.size * lines, dense.size * 2),
        name="gradients",
    )(ids, dense, column, slope, turned, class_weight_turned, class_bias, *terms)


def finish_kernel(features, lines, classes, ids, mine, other, loss_out, weight_out, bias_out, class_out, class_bias_out, packed):
    part = mine.shape[0]
    core = ids[0] & 1
    packed[pl.ds(pl.multiple_of(core * part, 8), part), :] = mine[...].astype(f32)
    packed[pl.ds(pl.multiple_of((1 - core) * part, 8), part), :] = other[...].astype(f32)
    tail = packed[pl.ds(features + lines + 8, 8), :]
    sums = jnp.sum(tail, axis=1, keepdims=True)
    members = sums[3:4]
    loss_out[...] = (sums[0:1] + sums[1:2] + sums[2:3]) / members
    weight_out[...] = packed[pl.ds(0, features), :] / members
    bias_out[...] = packed[pl.ds(features + lines - 1, 1), :] / members
    class_out[...] = packed[pl.ds(features, classes), :] / members
    class_bias_out[...] = packed[pl.ds(features + lines, 1), :][:, :classes] / members


def finish(ids, mine, other, features, lines, classes):
    part, width = mine.shape
    return pl.pallas_call(
        functools.partial(finish_kernel, features, lines, classes),
        out_shape=[
            jax.ShapeDtypeStruct((1, 1), f32),
            jax.ShapeDtypeStruct((features, width), f32),
            jax.ShapeDtypeStruct((1, width), f32),
            jax.ShapeDtypeStruct((classes, width), f32),
            jax.ShapeDtypeStruct((1, classes), f32),
        ],
        in_specs=[SMEM, VMEM, VMEM],
        out_specs=[VMEM] * 5,
        scratch_shapes=[pltpu.VMEM((2 * part, width), f32)],
        compiler_params=params(4 * MIB),
        name="finish",
    )(ids, mine, other)


def swap(value, axis, mask):
    size = lax.axis_size(axis)
    return lax.ppermute(value, axis, [(k, k ^ mask) for k in range(size)])


def gather_row(value):
    size = lax.axis_size("row")
    even = [value] + [swap(value, "row", k) for k in range(2, size, 2)]
    odd = [swap(even[0], "row", 1)]
    odd += [swap(piece, "row", 1) for piece in even[1:]]
    return even, odd


def sum_over(value, axis, low, high):
    while low < high:
        step = min(2, high - low)
        parts = [value.astype(WIRE)]
        parts += [swap(parts[0], axis, k << low) for k in range(1, 1 << step)]
        value = tree_sum(parts)
        low += step
    return value


def step(
    node_features,
    tile_values,
    tile_rows,
    tile_cols,
    tile_count,
    labels,
    train_mask,
    hidden_weight,
    hidden_bias,
    class_weight,
    class_bias,
):
    nodes, features = node_features.shape
    classes = class_weight.shape[1]
    n_row, n_col = lax.axis_size("row"), lax.axis_size("col")
    row_bits, col_bits = n_row.bit_length() - 1, n_col.bit_length() - 1
    lines = (classes // 16 + 1) * 16
    ids = jnp.stack([lax.axis_index("row"), lax.axis_index("col")]).astype(jnp.int32)
    code = (labels + MASK_CODE * train_mask).astype(f32)[None, :]
    bias = hidden_bias[None, :]
    class_turned = jnp.pad(class_weight.T, ((0, TILE - classes), (0, 0)))
    class_bias_lanes = jnp.pad(class_bias, (0, TILE - classes))[None, :]

    near, far = gather_row(node_features)
    total = collect(
        tile_values[0, 0], tile_rows[0], tile_cols[0], tile_count, n_col * nodes // TILE, n_row * nodes // TILE
    )
    dense, part = first_near(ids, total, near, n_col)
    terms = first_far(ids, dense, part, far, n_col)
    arrived = [terms[0]] + [swap(terms[k], "col", k) for k in range(1, n_col)]
    first_agg = tree_sum(arrived).astype(bf16)
    near, far = gather_row(first_agg)
    pieces = [piece for pair in zip(near, far) for piece in pair]
    hidden, column, term = hidden_terms(
        ids, dense, hidden_weight, bias, class_turned, code, pieces, n_col, lines
    )
    class_terms = [term] + [swap(term, "col", k) for k in range(1, n_col)]
    slope, turned = slopes(ids, hidden_weight, bias, pieces)
    logits, keep, send = gradients(
        ids, dense, column, slope, turned, class_turned, class_bias_lanes, class_terms, classes
    )
    part = keep.astype(f32) + swap(send, "row", 1).astype(f32)
    part = sum_over(part, "row", 1, row_bits)
    part = sum_over(part, "col", 0, col_bits)
    mine = part.astype(WIRE)
    other = swap(mine, "row", 1)
    loss, weight_grad, bias_grad, class_grad, class_bias_grad = finish(
        ids, mine, other, features, lines, classes
    )
    return (
        hidden,
        logits,
        loss[0, 0],
        weight_grad,
        bias_grad[0],
        class_grad.T,
        class_bias_grad[0],
    )


def solution(mesh):
    in_specs = (
        P(("row", "col"), None),
        P("row", "col", None, None, None),
        P("row", "col", None),
        P("row", "col", None),
        P("row", "col"),
        P(("row", "col")),
        P(("row", "col")),
        P(),
        P(),
        P(),
        P(),
    )
    out_specs = (P(("row", "col"), None), P(None, ("row", "col")), P(), P(), P(), P(), P())
    return jax.shard_map(step, mesh=mesh, in_specs=in_specs, out_specs=out_specs, check_vma=False)
```

profile of v0, /device:TPU:0, one launch (start us, length us, event | category | flops | bytes accessed | tf_op | source)
XLA Modules:
  0.0 74.0 jit_solution(12851694153138848947)
XLA Ops:
  0.6 3.0 %collective-permute-start = (bf16[256,128]{1,0:T(8,128)(2,1)}, bf16[256,128]{1,0:T(8,128)(2,1)S(1)}, u32[]{:S(2)}, u32[]{:S(2)}) collective-permute-start(bf16[256,128]{1,0:T(8,128)(2,1)} %refs_0_.1), channel_id=1, source_target_pairs={{0,8},{4,12},{8,0},{12,4},{16,24},{20,28},{24,16},{28,20},{1,9},{5... | collective-permute-start | bytes 196616 | tf_op jit(solution)/shard_map/ppermute | solution.py:400
  3.7 1.5 %collective-permute-start.1 = (bf16[256,128]{1,0:T(8,128)(2,1)}, bf16[256,128]{1,0:T(8,128)(2,1)S(1)}, u32[]{:S(2)}, u32[]{:S(2)}) collective-permute-start(bf16[256,128]{1,0:T(8,128)(2,1)} %refs_0_.1), channel_id=1, source_target_pairs={{0,16},{4,20},{8,24},{12,28},{16,0},{20,4},{24,8},{28,12},{1,17},{... | collective-permute-start | bytes 196616 | tf_op jit(solution)/shard_map/ppermute | solution.py:400
  5.2 0.0 collective-permute-start.2
  5.2 1.1 %collective-permute-done.refs_1_ = bf16[256,128]{1,0:T(8,128)(2,1)S(1)} collective-permute-done((bf16[256,128]{1,0:T(8,128)(2,1)}, bf16[256,128]{1,0:T(8,128)(2,1)S(1)}, u32[]{:S(2)}, u32[]{:S(2)}) %collective-permute-start) | collective-permute-done | bytes 65568 | tf_op jit(solution)/shard_map/ppermute | solution.py:400
  6.3 1.8 %collective-permute-done.1.refs_2_ = bf16[256,128]{1,0:T(8,128)(2,1)S(1)} collective-permute-done((bf16[256,128]{1,0:T(8,128)(2,1)}, bf16[256,128]{1,0:T(8,128)(2,1)S(1)}, u32[]{:S(2)}, u32[]{:S(2)}) %collective-permute-start.1) | collective-permute-done | bytes 65568 | tf_op jit(solution)/shard_map/ppermute | solution.py:400
  8.1 2.4 %collective-permute-done.2.refs_3_ = bf16[256,128]{1,0:T(8,128)(2,1)S(1)} collective-permute-done((bf16[256,128]{1,0:T(8,128)(2,1)}, bf16[256,128]{1,0:T(8,128)(2,1)S(1)}, u32[]{:S(2)}, u32[]{:S(2)}) %collective-permute-start.2) | collective-permute-done | bytes 65568 | tf_op jit(solution)/shard_map/ppermute | solution.py:400
  10.6 0.1 pad_add_fusion.ids
  11.3 0.0 copy-start
  11.3 1.9 %collect.1.total = f32[129,128,128]{2,1,0:T(8,128)S(1)} custom-call(s32[1,1]{1,0:T(1,128)S(6)} %copy.18.count, s32[1,384]{1,0:T(1,128)} %bitcast.19, s32[1,384]{1,0:T(1,128)} %bitcast.20, bf16[384,128,128]{2,1,0:T(8,128)(2,1)} %bitcast.17), custom_call_target="tpu_custom_call" | custom-call | flops 6291456 | bytes 12582912 | tf_op jit(solution)/shard_map/collect/pallas_call | solution.py:96
  13.3 2.1 %first_near.1 = (bf16[1024,2048]{1,0:T(8,128)(2,1)S(1)}, f32[1024,128]{1,0:T(8,128)S(1)}) custom-call(s32[2]{0:T(128)S(1)} %pad_add_fusion.ids, f32[129,128,128]{2,1,0:T(8,128)S(1)} %collect.1.total, bf16[256,128]{1,0:T(8,128)(2,1)S(1)} %copy-done, bf16[256,128]{1,0:T(8,128)(2,1)S(1)} %collective-permute-done.refs_1_, ...), custom_call_target="tpu_custom_call" | custom-call | flops 268435456 | bytes 12582912 | tf_op jit(solution)/shard_map/first_near/pallas_call | solution.py:158
  15.5 1.3 %first_far.1 = (bf16[256,128]{1,0:T(8,128)(2,1)S(1)}, bf16[256,128]{1,0:T(8,128)(2,1)S(1)}, bf16[256,128]{1,0:T(8,128)(2,1)S(1)}, bf16[256,128]{1,0:T(8,128)(2,1)S(1)}) custom-call(s32[2]{0:T(128)S(1)} %pad_add_fusion.ids, bf16[1024,2048]{1,0:T(8,128)(2,1)S(1)} %get-tuple-element.26.dense, f32[1024,128]{1,0:T(8,128)S(1)} %get-tuple-element.27.part, ...), custom_call_target="tpu_custom_call" | custom-call | flops 268435456 | bytes 2097152 | tf_op jit(solution)/shard_map/first_far/pallas_call | solution.py:185
  16.8 1.6 %collective-permute-start.7 = (bf16[256,128]{1,0:T(8,128)(2,1)S(1)}, bf16[256,128]{1,0:T(8,128)(2,1)S(1)}, u32[]{:S(2)}, u32[]{:S(2)}) collective-permute-start(bf16[256,128]{1,0:T(8,128)(2,1)S(1)} %get-tuple-element.29), channel_id=1, source_target_pairs={{0,1},{1,0},{2,3},{3,2},{4,5},{5,4},{6,7},{7,6},{8,9},{9,8},{10,11... | collective-permute-start | bytes 196616 | tf_op jit(solution)/shard_map/ppermute | solution.py:400
  18.4 3.2 %collective-permute-start.8 = (bf16[256,128]{1,0:T(8,128)(2,1)S(1)}, bf16[256,128]{1,0:T(8,128)(2,1)S(1)}, u32[]{:S(2)}, u32[]{:S(2)}) collective-permute-start(bf16[256,128]{1,0:T(8,128)(2,1)S(1)} %get-tuple-element.30), channel_id=1, source_target_pairs={{0,2},{1,3},{2,0},{3,1},{4,6},{5,7},{6,4},{7,5},{8,10},{9,11},{10,... | collective-permute-start | bytes 196616 | tf_op jit(solution)/shard_map/ppermute | solution.py:400
  21.6 0.0 collective-permute-start.9
  21.7 4.3 %collective-permute-done.8 = bf16[256,128]{1,0:T(8,128)(2,1)S(1)} collective-permute-done((bf16[256,128]{1,0:T(8,128)(2,1)S(1)}, bf16[256,128]{1,0:T(8,128)(2,1)S(1)}, u32[]{:S(2)}, u32[]{:S(2)}) %collective-permute-start.8) | collective-permute-done | bytes 65568 | tf_op jit(solution)/shard_map/ppermute | solution.py:400
  26.0 1.8 %collective-permute-done.9 = bf16[256,128]{1,0:T(8,128)(2,1)S(1)} collective-permute-done((bf16[256,128]{1,0:T(8,128)(2,1)S(1)}, bf16[256,128]{1,0:T(8,128)(2,1)S(1)}, u32[]{:S(2)}, u32[]{:S(2)}) %collective-permute-start.9) | collective-permute-done | bytes 65568 | tf_op jit(solution)/shard_map/ppermute | solution.py:400
  27.8 0.9 %collective-permute-start.11 = (bf16[256,128]{1,0:T(8,128)(2,1)S(1)}, bf16[256,128]{1,0:T(8,128)(2,1)S(1)}, u32[]{:S(2)}, u32[]{:S(2)}) collective-permute-start(bf16[256,128]{1,0:T(8,128)(2,1)S(1)} %add_convert_fusion.refs_0_), channel_id=1, source_target_pairs={{0,8},{4,12},{8,0},{12,4},{16,24},{20,28},{24,16},{28,20},{1,9},{5... | collective-permute-start | bytes 196616 | tf_op jit(solution)/shard_map/ppermute | solution.py:400
  28.7 0.4 collective-permute-start.13
  29.1 2.3 %collective-permute-start.15 = (bf16[256,128]{1,0:T(8,128)(2,1)S(1)}, bf16[256,128]{1,0:T(8,128)(2,1)S(1)}, u32[]{:S(2)}, u32[]{:S(2)}) collective-permute-start(bf16[256,128]{1,0:T(8,128)(2,1)S(1)} %add_convert_fusion.refs_0_), channel_id=1, source_target_pairs={{0,24},{4,28},{8,16},{12,20},{16,8},{20,12},{24,0},{28,4},{1,25},{... | collective-permute-start | bytes 196616 | tf_op jit(solution)/shard_map/ppermute | solution.py:400
  31.4 1.3 %collective-permute-done.11.refs_2_ = bf16[256,128]{1,0:T(8,128)(2,1)S(1)} collective-permute-done((bf16[256,128]{1,0:T(8,128)(2,1)S(1)}, bf16[256,128]{1,0:T(8,128)(2,1)S(1)}, u32[]{:S(2)}, u32[]{:S(2)}) %collective-permute-start.11) | collective-permute-done | bytes 65568 | tf_op jit(solution)/shard_map/ppermute | solution.py:400
  32.7 1.7 %collective-permute-done.13.refs_4_ = bf16[256,128]{1,0:T(8,128)(2,1)S(1)} collective-permute-done((bf16[256,128]{1,0:T(8,128)(2,1)S(1)}, bf16[256,128]{1,0:T(8,128)(2,1)S(1)}, u32[]{:S(2)}, u32[]{:S(2)}) %collective-permute-start.13) | collective-permute-done | bytes 65568 | tf_op jit(solution)/shard_map/ppermute | solution.py:400
  34.4 0.5 collective-permute-start.16
  35.0 0.7 collective-permute-done.14.refs_5_
  35.6 0.2 collective-permute-done.16.refs_7_
  35.8 3.3 %hidden_terms.1 = (bf16[256,256]{1,0:T(8,128)(2,1)}, bf16[2048,256]{1,0:T(8,128)(2,1)S(1)}, bf16[48,1024]{1,0:T(8,128)(2,1)S(1)}) custom-call(s32[2]{0:T(128)S(1)} %pad_add_fusion.ids, bf16[1024,2048]{1,0:T(8,128)(2,1)S(1)} %get-tuple-element.26.dense, bf16[128,256]{1,0:T(8,128)(2,1)S(1)} %copy-done.1, f32[1,256]{1,0:T(1,128)S(1)} %bitcast.15, ...), custom_call_target="tpu_custom_call" | custom-call | flops 1073741824 | bytes 4194304 | tf_op jit(solution)/shard_map/hidden_terms/pallas_call | solution.py:226
  39.1 0.8 %collective-permute-start.17 = (bf16[48,1024]{1,0:T(8,128)(2,1)S(1)}, bf16[48,1024]{1,0:T(8,128)(2,1)S(1)}, u32[]{:S(2)}, u32[]{:S(2)}) collective-permute-start(bf16[48,1024]{1,0:T(8,128)(2,1)S(1)} %get-tuple-element.36.refs_0_), channel_id=1, source_target_pairs={{0,1},{1,0},{2,3},{3,2},{4,5},{5,4},{6,7},{7,6},{8,9},{9,8},{10,11... | collective-permute-start | bytes 294920 | tf_op jit(solution)/shard_map/ppermute | solution.py:400
  39.9 1.9 %collective-permute-start.18 = (bf16[48,1024]{1,0:T(8,128)(2,1)S(1)}, bf16[48,1024]{1,0:T(8,128)(2,1)S(1)}, u32[]{:S(2)}, u32[]{:S(2)}) collective-permute-start(bf16[48,1024]{1,0:T(8,128)(2,1)S(1)} %get-tuple-element.36.refs_0_), channel_id=1, source_target_pairs={{0,2},{1,3},{2,0},{3,1},{4,6},{5,7},{6,4},{7,5},{8,10},{9,11},{10,... | collective-permute-start | bytes 294920 | tf_op jit(solution)/shard_map/ppermute | solution.py:400
  41.8 1.7 %collective-permute-start.19 = (bf16[48,1024]{1,0:T(8,128)(2,1)S(1)}, bf16[48,1024]{1,0:T(8,128)(2,1)S(1)}, u32[]{:S(2)}, u32[]{:S(2)}) collective-permute-start(bf16[48,1024]{1,0:T(8,128)(2,1)S(1)} %get-tuple-element.36.refs_0_), channel_id=1, source_target_pairs={{0,3},{1,2},{2,1},{3,0},{4,7},{5,6},{6,5},{7,4},{8,11},{9,10},{10,... | collective-permute-start | bytes 294920 | tf_op jit(solution)/shard_map/ppermute | solution.py:400
  43.5 1.5 %slopes.1 = (f32[2048,256]{1,0:T(8,128)S(1)}, bf16[128,2048]{1,0:T(8,128)(2,1)S(1)}) custom-call(s32[2]{0:T(128)S(1)} %pad_add_fusion.ids, bf16[128,256]{1,0:T(8,128)(2,1)S(1)} %copy-done.1, f32[1,256]{1,0:T(1,128)S(1)} %bitcast.16, bf16[256,128]{1,0:T(8,128)(2,1)S(1)} %add_convert_fusion.refs_0_, bf16[256,128]{1,0:T(8,128)(2,1)S(1)} %collective-permute-done.10.refs_1_, ...), custom_call_target="tpu_custom_call" | custom-call | flops 134217728 | bytes 2097152 | tf_op jit(solution)/shard_map/slopes/pallas_call | solution.py:260
  45.0 0.8 %collective-permute-done.17.refs_1_ = bf16[48,1024]{1,0:T(8,128)(2,1)S(1)} collective-permute-done((bf16[48,1024]{1,0:T(8,128)(2,1)S(1)}, bf16[48,1024]{1,0:T(8,128)(2,1)S(1)}, u32[]{:S(2)}, u32[]{:S(2)}) %collective-permute-start.17) | collective-permute-done | bytes 98336 | tf_op jit(solution)/shard_map/ppermute | solution.py:400
  45.8 4.6 %collective-permute-done.18.refs_2_ = bf16[48,1024]{1,0:T(8,128)(2,1)S(1)} collective-permute-done((bf16[48,1024]{1,0:T(8,128)(2,1)S(1)}, bf16[48,1024]{1,0:T(8,128)(2,1)S(1)}, u32[]{:S(2)}, u32[]{:S(2)}) %collective-permute-start.18) | collective-permute-done | bytes 98336 | tf_op jit(solution)/shard_map/ppermute | solution.py:400
  50.4 2.5 %gradients.1 = (f32[47,256]{1,0:T(8,128)}, bf16[96,256]{1,0:T(8,128)(2,1)S(1)}, bf16[96,256]{1,0:T(8,128)(2,1)S(1)}) custom-call(s32[2]{0:T(128)S(1)} %pad_add_fusion.ids, bf16[1024,2048]{1,0:T(8,128)(2,1)S(1)} %get-tuple-element.26.dense, bf16[2048,256]{1,0:T(8,128)(2,1)S(1)} %get-tuple-element.33.column, f32[2048,256]{1,0:T(8,128)S(1)} %get-tuple-element.34.slope, ...), custom_call_target="tpu_custom_call" | custom-call | flops 402653184 | bytes 4194304 | tf_op jit(solution)/shard_map/gradients/pallas_call | solution.py:345
  52.8 0.1 collective-permute-start.20
  52.9 1.2 %collective-permute-done.20 = bf16[96,256]{1,0:T(8,128)(2,1)S(1)} collective-permute-done((bf16[96,256]{1,0:T(8,128)(2,1)S(1)}, bf16[96,256]{1,0:T(8,128)(2,1)S(1)}, u32[]{:S(2)}, u32[]{:S(2)}) %collective-permute-start.20) | collective-permute-done | bytes 49184 | tf_op jit(solution)/shard_map/ppermute | solution.py:400
  54.1 2.2 %collective-permute-start.21 = (bf16[96,256]{1,0:T(8,128)(2,1)S(1)}, bf16[96,256]{1,0:T(8,128)(2,1)S(1)}, u32[]{:S(2)}, u32[]{:S(2)}) collective-permute-start(bf16[96,256]{1,0:T(8,128)(2,1)S(1)} %add_convert_fusion.3), channel_id=1, source_target_pairs={{0,8},{4,12},{8,0},{12,4},{16,24},{20,28},{24,16},{28,20},{1,9},{5... | collective-permute-start | bytes 147464 | tf_op jit(solution)/shard_map/ppermute | solution.py:400
  56.4 1.2 %collective-permute-start.22 = (bf16[96,256]{1,0:T(8,128)(2,1)S(1)}, bf16[96,256]{1,0:T(8,128)(2,1)S(1)}, u32[]{:S(2)}, u32[]{:S(2)}) collective-permute-start(bf16[96,256]{1,0:T(8,128)(2,1)S(1)} %add_convert_fusion.3), channel_id=1, source_target_pairs={{0,16},{4,20},{8,24},{12,28},{16,0},{20,4},{24,8},{28,12},{1,17},{... | collective-permute-start | bytes 147464 | tf_op jit(solution)/shard_map/ppermute | solution.py:400
  57.6 0.3 collective-permute-start.23
  57.9 0.5 collective-permute-done.21
  58.5 2.0 %collective-permute-done.22 = bf16[96,256]{1,0:T(8,128)(2,1)S(1)} collective-permute-done((bf16[96,256]{1,0:T(8,128)(2,1)S(1)}, bf16[96,256]{1,0:T(8,128)(2,1)S(1)}, u32[]{:S(2)}, u32[]{:S(2)}) %collective-permute-start.22) | collective-permute-done | bytes 49184 | tf_op jit(solution)/shard_map/ppermute | solution.py:400
  60.5 2.1 %collective-permute-done.23 = bf16[96,256]{1,0:T(8,128)(2,1)S(1)} collective-permute-done((bf16[96,256]{1,0:T(8,128)(2,1)S(1)}, bf16[96,256]{1,0:T(8,128)(2,1)S(1)}, u32[]{:S(2)}, u32[]{:S(2)}) %collective-permute-start.23) | collective-permute-done | bytes 49184 | tf_op jit(solution)/shard_map/ppermute | solution.py:400
  62.6 1.8 %collective-permute-start.24 = (bf16[96,256]{1,0:T(8,128)(2,1)S(1)}, bf16[96,256]{1,0:T(8,128)(2,1)S(1)}, u32[]{:S(2)}, u32[]{:S(2)}) collective-permute-start(bf16[96,256]{1,0:T(8,128)(2,1)S(1)} %add_convert_fusion.2), channel_id=1, source_target_pairs={{0,1},{1,0},{2,3},{3,2},{4,5},{5,4},{6,7},{7,6},{8,9},{9,8},{10,11... | collective-permute-start | bytes 147464 | tf_op jit(solution)/shard_map/ppermute | solution.py:400
  64.4 1.0 %collective-permute-start.25 = (bf16[96,256]{1,0:T(8,128)(2,1)S(1)}, bf16[96,256]{1,0:T(8,128)(2,1)S(1)}, u32[]{:S(2)}, u32[]{:S(2)}) collective-permute-start(bf16[96,256]{1,0:T(8,128)(2,1)S(1)} %add_convert_fusion.2), channel_id=1, source_target_pairs={{0,2},{1,3},{2,0},{3,1},{4,6},{5,7},{6,4},{7,5},{8,10},{9,11},{10,... | collective-permute-start | bytes 147464 | tf_op jit(solution)/shard_map/ppermute | solution.py:400
  65.4 1.7 %collective-permute-start.26 = (bf16[96,256]{1,0:T(8,128)(2,1)S(1)}, bf16[96,256]{1,0:T(8,128)(2,1)S(1)}, u32[]{:S(2)}, u32[]{:S(2)}) collective-permute-start(bf16[96,256]{1,0:T(8,128)(2,1)S(1)} %add_convert_fusion.2), channel_id=1, source_target_pairs={{0,3},{1,2},{2,1},{3,0},{4,7},{5,6},{6,5},{7,4},{8,11},{9,10},{10,... | collective-permute-start | bytes 147464 | tf_op jit(solution)/shard_map/ppermute | solution.py:400
  67.1 2.8 %collective-permute-done.25 = bf16[96,256]{1,0:T(8,128)(2,1)S(1)} collective-permute-done((bf16[96,256]{1,0:T(8,128)(2,1)S(1)}, bf16[96,256]{1,0:T(8,128)(2,1)S(1)}, u32[]{:S(2)}, u32[]{:S(2)}) %collective-permute-start.25) | collective-permute-done | bytes 49184 | tf_op jit(solution)/shard_map/ppermute | solution.py:400
  69.9 1.5 %collective-permute-done.26 = bf16[96,256]{1,0:T(8,128)(2,1)S(1)} collective-permute-done((bf16[96,256]{1,0:T(8,128)(2,1)S(1)}, bf16[96,256]{1,0:T(8,128)(2,1)S(1)}, u32[]{:S(2)}, u32[]{:S(2)}) %collective-permute-start.26) | collective-permute-done | bytes 49184 | tf_op jit(solution)/shard_map/ppermute | solution.py:400
  71.4 0.1 collective-permute-start.27
  71.5 1.2 %collective-permute-done.27.other = bf16[96,256]{1,0:T(8,128)(2,1)S(1)} collective-permute-done((bf16[96,256]{1,0:T(8,128)(2,1)S(1)}, bf16[96,256]{1,0:T(8,128)(2,1)S(1)}, u32[]{:S(2)}, u32[]{:S(2)}) %collective-permute-start.27) | collective-permute-done | bytes 49184 | tf_op jit(solution)/shard_map/ppermute | solution.py:400
  72.7 1.3 %finish.1 = (f32[1,1]{1,0:T(1,128)}, f32[128,256]{1,0:T(8,128)}, f32[1,256]{1,0:T(1,128)}, f32[47,256]{1,0:T(8,128)}, f32[1,47]{1,0:T(1,128)}) custom-call(s32[2]{0:T(128)S(1)} %pad_add_fusion.ids, bf16[96,256]{1,0:T(8,128)(2,1)S(1)} %add_convert_fusion.1.mine, bf16[96,256]{1,0:T(8,128)(2,1)S(1)} %collective-permute-done.27.other), custom_call_target="tpu_custom_call" | custom-call | tf_op jit(solution)/shard_map/finish/pallas_call | solution.py:381
  (37 shorter events, 0.2 us)
Async XLA Ops:
  0.6 5.7 %collective-permute-start = (bf16[256,128]{1,0:T(8,128)(2,1)}, bf16[256,128]{1,0:T(8,128)(2,1)S(1)}, u32[]{:S(2)}, u32[]{:S(2)}) collective-permute-start(bf16[256,128]{1,0:T(8,128)(2,1)} %refs_0_.1), channel_id=1, source_target_pairs={{0,8},{4,12},{8,0},{12,4},{16,24},{20,28},{24,16},{28,20},{1,9},{5... | collective-permute-start | bytes 196616 | tf_op jit(solution)/shard_map/ppermute | solution.py:400
  3.7 4.5 %collective-permute-start.1 = (bf16[256,128]{1,0:T(8,128)(2,1)}, bf16[256,128]{1,0:T(8,128)(2,1)S(1)}, u32[]{:S(2)}, u32[]{:S(2)}) collective-permute-start(bf16[256,128]{1,0:T(8,128)(2,1)} %refs_0_.1), channel_id=1, source_target_pairs={{0,16},{4,20},{8,24},{12,28},{16,0},{20,4},{24,8},{28,12},{1,17},{... | collective-permute-start | bytes 196616 | tf_op jit(solution)/shard_map/ppermute | solution.py:400
  5.2 5.4 %collective-permute-start.2 = (bf16[256,128]{1,0:T(8,128)(2,1)}, bf16[256,128]{1,0:T(8,128)(2,1)S(1)}, u32[]{:S(2)}, u32[]{:S(2)}) collective-permute-start(bf16[256,128]{1,0:T(8,128)(2,1)} %refs_0_.1), channel_id=1, source_target_pairs={{0,24},{4,28},{8,16},{12,20},{16,8},{20,12},{24,0},{28,4},{1,25},{... | collective-permute-start | bytes 196616 | tf_op jit(solution)/shard_map/ppermute | solution.py:400
  5.2 10.2 %collective-permute-start.3 = (bf16[256,128]{1,0:T(8,128)(2,1)}, bf16[256,128]{1,0:T(8,128)(2,1)S(1)}, u32[]{:S(2)}, u32[]{:S(2)}) collective-permute-start(bf16[256,128]{1,0:T(8,128)(2,1)} %refs_0_.1), channel_id=1, source_target_pairs={{0,4},{4,0},{8,12},{12,8},{16,20},{20,16},{24,28},{28,24},{1,5},{5... | collective-permute-start | bytes 196616 | tf_op jit(solution)/shard_map/ppermute | solution.py:400
  6.3 9.1 %collective-permute-start.4 = (bf16[256,128]{1,0:T(8,128)(2,1)S(1)}, bf16[256,128]{1,0:T(8,128)(2,1)S(1)}, u32[]{:S(2)}, u32[]{:S(2)}) collective-permute-start(bf16[256,128]{1,0:T(8,128)(2,1)S(1)} %collective-permute-done.refs_1_), channel_id=1, source_target_pairs={{0,4},{4,0},{8,12},{12,8},{16,20},{20,16},{24,28},{28,24},{1,5},{5... | collective-permute-start | bytes 196616 | tf_op jit(solution)/shard_map/ppermute | solution.py:400
  8.1 7.3 %collective-permute-start.5 = (bf16[256,128]{1,0:T(8,128)(2,1)S(1)}, bf16[256,128]{1,0:T(8,128)(2,1)S(1)}, u32[]{:S(2)}, u32[]{:S(2)}) collective-permute-start(bf16[256,128]{1,0:T(8,128)(2,1)S(1)} %collective-permute-done.1.refs_2_), channel_id=1, source_target_pairs={{0,4},{4,0},{8,12},{12,8},{16,20},{20,16},{24,28},{28,24},{1,5},{5... | collective-permute-start | bytes 196616 | tf_op jit(solution)/shard_map/ppermute | solution.py:400
  10.6 4.9 %collective-permute-start.6 = (bf16[256,128]{1,0:T(8,128)(2,1)S(1)}, bf16[256,128]{1,0:T(8,128)(2,1)S(1)}, u32[]{:S(2)}, u32[]{:S(2)}) collective-permute-start(bf16[256,128]{1,0:T(8,128)(2,1)S(1)} %collective-permute-done.2.refs_3_), channel_id=1, source_target_pairs={{0,4},{4,0},{8,12},{12,8},{16,20},{20,16},{24,28},{28,24},{1,5},{5... | collective-permute-start | bytes 196616 | tf_op jit(solution)/shard_map/ppermute | solution.py:400
  11.3 2.0 %copy-start = (bf16[256,128]{1,0:T(8,128)(2,1)S(1)}, bf16[256,128]{1,0:T(8,128)(2,1)}, u32[]{:S(2)}) copy-start(bf16[256,128]{1,0:T(8,128)(2,1)} %refs_0_.1) | copy-start | bytes 196612
  13.2 21.6 %copy-start.4 = (s32[256]{0:T(256)S(1)}, s32[256]{0:T(256)}, u32[]{:S(2)}) copy-start(s32[256]{0:T(256)} %param.16) | copy-start | bytes 3076
  13.3 21.6 %copy-start.5 = (s32[256]{0:T(256)S(1)}, s32[256]{0:T(256)}, u32[]{:S(2)}) copy-start(s32[256]{0:T(256)} %param.17) | copy-start | bytes 3076
  13.3 21.6 %copy-start.3 = (bf16[256,47]{0,1:T(8,128)(2,1)S(1)}, bf16[256,47]{0,1:T(8,128)(2,1)}, u32[]{:S(2)}) copy-start(bf16[256,47]{0,1:T(8,128)(2,1)} %param.20) | copy-start | bytes 72196
  13.3 22.5 %copy-start.1 = (bf16[128,256]{1,0:T(8,128)(2,1)S(1)}, bf16[128,256]{1,0:T(8,128)(2,1)}, u32[]{:S(2)}) copy-start(bf16[128,256]{1,0:T(8,128)(2,1)} %weight.3) | copy-start | bytes 196612
  13.3 22.5 %copy-start.2 = (f32[256]{0:T(256)S(1)}, f32[256]{0:T(256)}, u32[]{:S(2)}) copy-start(f32[256]{0:T(256)} %param.19) | copy-start | bytes 3076
  13.3 30.2 %copy-start.6 = (f32[47]{0:T(128)S(1)}, f32[47]{0:T(128)}, u32[]{:S(2)}) copy-start(f32[47]{0:T(128)} %param.21) | copy-start | bytes 568
  16.8 4.9 %collective-permute-start.7 = (bf16[256,128]{1,0:T(8,128)(2,1)S(1)}, bf16[256,128]{1,0:T(8,128)(2,1)S(1)}, u32[]{:S(2)}, u32[]{:S(2)}) collective-permute-start(bf16[256,128]{1,0:T(8,128)(2,1)S(1)} %get-tuple-element.29), channel_id=1, source_target_pairs={{0,1},{1,0},{2,3},{3,2},{4,5},{5,4},{6,7},{7,6},{8,9},{9,8},{10,11... | collective-permute-start | bytes 196616 | tf_op jit(solution)/shard_map/ppermute | solution.py:400
  18.4 7.6 %collective-permute-start.8 = (bf16[256,128]{1,0:T(8,128)(2,1)S(1)}, bf16[256,128]{1,0:T(8,128)(2,1)S(1)}, u32[]{:S(2)}, u32[]{:S(2)}) collective-permute-start(bf16[256,128]{1,0:T(8,128)(2,1)S(1)} %get-tuple-element.30), channel_id=1, source_target_pairs={{0,2},{1,3},{2,0},{3,1},{4,6},{5,7},{6,4},{7,5},{8,10},{9,11},{10,... | collective-permute-start | bytes 196616 | tf_op jit(solution)/shard_map/ppermute | solution.py:400
  21.6 6.2 %collective-permute-start.9 = (bf16[256,128]{1,0:T(8,128)(2,1)S(1)}, bf16[256,128]{1,0:T(8,128)(2,1)S(1)}, u32[]{:S(2)}, u32[]{:S(2)}) collective-permute-start(bf16[256,128]{1,0:T(8,128)(2,1)S(1)} %get-tuple-element.31), channel_id=1, source_target_pairs={{0,3},{1,2},{2,1},{3,0},{4,7},{5,6},{6,5},{7,4},{8,11},{9,10},{10,... | collective-permute-start | bytes 196616 | tf_op jit(solution)/shard_map/ppermute | solution.py:400
  27.8 4.9 %collective-permute-start.11 = (bf16[256,128]{1,0:T(8,128)(2,1)S(1)}, bf16[256,128]{1,0:T(8,128)(2,1)S(1)}, u32[]{:S(2)}, u32[]{:S(2)}) collective-permute-start(bf16[256,128]{1,0:T(8,128)(2,1)S(1)} %add_convert_fusion.refs_0_), channel_id=1, source_target_pairs={{0,8},{4,12},{8,0},{12,4},{16,24},{20,28},{24,16},{28,20},{1,9},{5... | collective-permute-start | bytes 196616 | tf_op jit(solution)/shard_map/ppermute | solution.py:400
  28.7 5.7 %collective-permute-start.13 = (bf16[256,128]{1,0:T(8,128)(2,1)S(1)}, bf16[256,128]{1,0:T(8,128)(2,1)S(1)}, u32[]{:S(2)}, u32[]{:S(2)}) collective-permute-start(bf16[256,128]{1,0:T(8,128)(2,1)S(1)} %add_convert_fusion.refs_0_), channel_id=1, source_target_pairs={{0,16},{4,20},{8,24},{12,28},{16,0},{20,4},{24,8},{28,12},{1,17},{... | collective-permute-start | bytes 196616 | tf_op jit(solution)/shard_map/ppermute | solution.py:400
  29.1 5.3 %collective-permute-start.15 = (bf16[256,128]{1,0:T(8,128)(2,1)S(1)}, bf16[256,128]{1,0:T(8,128)(2,1)S(1)}, u32[]{:S(2)}, u32[]{:S(2)}) collective-permute-start(bf16[256,128]{1,0:T(8,128)(2,1)S(1)} %add_convert_fusion.refs_0_), channel_id=1, source_target_pairs={{0,24},{4,28},{8,16},{12,20},{16,8},{20,12},{24,0},{28,4},{1,25},{... | collective-permute-start | bytes 196616 | tf_op jit(solution)/shard_map/ppermute | solution.py:400
  31.4 3.6 %collective-permute-start.10 = (bf16[256,128]{1,0:T(8,128)(2,1)S(1)}, bf16[256,128]{1,0:T(8,128)(2,1)S(1)}, u32[]{:S(2)}, u32[]{:S(2)}) collective-permute-start(bf16[256,128]{1,0:T(8,128)(2,1)S(1)} %add_convert_fusion.refs_0_), channel_id=1, source_target_pairs={{0,4},{4,0},{8,12},{12,8},{16,20},{20,16},{24,28},{28,24},{1,5},{5... | collective-permute-start | bytes 196616 | tf_op jit(solution)/shard_map/ppermute | solution.py:400
  32.7 2.3 %collective-permute-start.12 = (bf16[256,128]{1,0:T(8,128)(2,1)S(1)}, bf16[256,128]{1,0:T(8,128)(2,1)S(1)}, u32[]{:S(2)}, u32[]{:S(2)}) collective-permute-start(bf16[256,128]{1,0:T(8,128)(2,1)S(1)} %collective-permute-done.11.refs_2_), channel_id=1, source_target_pairs={{0,4},{4,0},{8,12},{12,8},{16,20},{20,16},{24,28},{28,24},{1,5},{5... | collective-permute-start | bytes 196616 | tf_op jit(solution)/shard_map/ppermute | solution.py:400
  34.4 1.3 %collective-permute-start.14 = (bf16[256,128]{1,0:T(8,128)(2,1)S(1)}, bf16[256,128]{1,0:T(8,128)(2,1)S(1)}, u32[]{:S(2)}, u32[]{:S(2)}) collective-permute-start(bf16[256,128]{1,0:T(8,128)(2,1)S(1)} %collective-permute-done.13.refs_4_), channel_id=1, source_target_pairs={{0,4},{4,0},{8,12},{12,8},{16,20},{20,16},{24,28},{28,24},{1,5},{5... | collective-permute-start | bytes 196616 | tf_op jit(solution)/shard_map/ppermute | solution.py:400
  34.4 1.4 %collective-permute-start.16 = (bf16[256,128]{1,0:T(8,128)(2,1)S(1)}, bf16[256,128]{1,0:T(8,128)(2,1)S(1)}, u32[]{:S(2)}, u32[]{:S(2)}) collective-permute-start(bf16[256,128]{1,0:T(8,128)(2,1)S(1)} %collective-permute-done.15.refs_6_), channel_id=1, source_target_pairs={{0,4},{4,0},{8,12},{12,8},{16,20},{20,16},{24,28},{28,24},{1,5},{5... | collective-permute-start | bytes 196616 | tf_op jit(solution)/shard_map/ppermute | solution.py:400
  39.1 6.7 %collective-permute-start.17 = (bf16[48,1024]{1,0:T(8,128)(2,1)S(1)}, bf16[48,1024]{1,0:T(8,128)(2,1)S(1)}, u32[]{:S(2)}, u32[]{:S(2)}) collective-permute-start(bf16[48,1024]{1,0:T(8,128)(2,1)S(1)} %get-tuple-element.36.refs_0_), channel_id=1, source_target_pairs={{0,1},{1,0},{2,3},{3,2},{4,5},{5,4},{6,7},{7,6},{8,9},{9,8},{10,11... | collective-permute-start | bytes 294920 | tf_op jit(solution)/shard_map/ppermute | solution.py:400
  39.9 10.4 %collective-permute-start.18 = (bf16[48,1024]{1,0:T(8,128)(2,1)S(1)}, bf16[48,1024]{1,0:T(8,128)(2,1)S(1)}, u32[]{:S(2)}, u32[]{:S(2)}) collective-permute-start(bf16[48,1024]{1,0:T(8,128)(2,1)S(1)} %get-tuple-element.36.refs_0_), channel_id=1, source_target_pairs={{0,2},{1,3},{2,0},{3,1},{4,6},{5,7},{6,4},{7,5},{8,10},{9,11},{10,... | collective-permute-start | bytes 294920 | tf_op jit(solution)/shard_map/ppermute | solution.py:400
  41.8 8.6 %collective-permute-start.19 = (bf16[48,1024]{1,0:T(8,128)(2,1)S(1)}, bf16[48,1024]{1,0:T(8,128)(2,1)S(1)}, u32[]{:S(2)}, u32[]{:S(2)}) collective-permute-start(bf16[48,1024]{1,0:T(8,128)(2,1)S(1)} %get-tuple-element.36.refs_0_), channel_id=1, source_target_pairs={{0,3},{1,2},{2,1},{3,0},{4,7},{5,6},{6,5},{7,4},{8,11},{9,10},{10,... | collective-permute-start | bytes 294920 | tf_op jit(solution)/shard_map/ppermute | solution.py:400
  52.8 1.3 %collective-permute-start.20 = (bf16[96,256]{1,0:T(8,128)(2,1)S(1)}, bf16[96,256]{1,0:T(8,128)(2,1)S(1)}, u32[]{:S(2)}, u32[]{:S(2)}) collective-permute-start(bf16[96,256]{1,0:T(8,128)(2,1)S(1)} %get-tuple-element.39), channel_id=1, source_target_pairs={{0,4},{4,0},{8,12},{12,8},{16,20},{20,16},{24,28},{28,24},{1,5},{5... | collective-permute-start | bytes 147464 | tf_op jit(solution)/shard_map/ppermute | solution.py:400
  54.1 4.3 %collective-permute-start.21 = (bf16[96,256]{1,0:T(8,128)(2,1)S(1)}, bf16[96,256]{1,0:T(8,128)(2,1)S(1)}, u32[]{:S(2)}, u32[]{:S(2)}) collective-permute-start(bf16[96,256]{1,0:T(8,128)(2,1)S(1)} %add_convert_fusion.3), channel_id=1, source_target_pairs={{0,8},{4,12},{8,0},{12,4},{16,24},{20,28},{24,16},{28,20},{1,9},{5... | collective-permute-start | bytes 147464 | tf_op jit(solution)/shard_map/ppermute | solution.py:400
  56.4 4.1 %collective-permute-start.22 = (bf16[96,256]{1,0:T(8,128)(2,1)S(1)}, bf16[96,256]{1,0:T(8,128)(2,1)S(1)}, u32[]{:S(2)}, u32[]{:S(2)}) collective-permute-start(bf16[96,256]{1,0:T(8,128)(2,1)S(1)} %add_convert_fusion.3), channel_id=1, source_target_pairs={{0,16},{4,20},{8,24},{12,28},{16,0},{20,4},{24,8},{28,12},{1,17},{... | collective-permute-start | bytes 147464 | tf_op jit(solution)/shard_map/ppermute | solution.py:400
  57.6 5.0 %collective-permute-start.23 = (bf16[96,256]{1,0:T(8,128)(2,1)S(1)}, bf16[96,256]{1,0:T(8,128)(2,1)S(1)}, u32[]{:S(2)}, u32[]{:S(2)}) collective-permute-start(bf16[96,256]{1,0:T(8,128)(2,1)S(1)} %add_convert_fusion.3), channel_id=1, source_target_pairs={{0,24},{4,28},{8,16},{12,20},{16,8},{20,12},{24,0},{28,4},{1,25},{... | collective-permute-start | bytes 147464 | tf_op jit(solution)/shard_map/ppermute | solution.py:400
  62.6 4.5 %collective-permute-start.24 = (bf16[96,256]{1,0:T(8,128)(2,1)S(1)}, bf16[96,256]{1,0:T(8,128)(2,1)S(1)}, u32[]{:S(2)}, u32[]{:S(2)}) collective-permute-start(bf16[96,256]{1,0:T(8,128)(2,1)S(1)} %add_convert_fusion.2), channel_id=1, source_target_pairs={{0,1},{1,0},{2,3},{3,2},{4,5},{5,4},{6,7},{7,6},{8,9},{9,8},{10,11... | collective-permute-start | bytes 147464 | tf_op jit(solution)/shard_map/ppermute | solution.py:400
  64.4 5.5 %collective-permute-start.25 = (bf16[96,256]{1,0:T(8,128)(2,1)S(1)}, bf16[96,256]{1,0:T(8,128)(2,1)S(1)}, u32[]{:S(2)}, u32[]{:S(2)}) collective-permute-start(bf16[96,256]{1,0:T(8,128)(2,1)S(1)} %add_convert_fusion.2), channel_id=1, source_target_pairs={{0,2},{1,3},{2,0},{3,1},{4,6},{5,7},{6,4},{7,5},{8,10},{9,11},{10,... | collective-permute-start | bytes 147464 | tf_op jit(solution)/shard_map/ppermute | solution.py:400
  65.4 6.0 %collective-permute-start.26 = (bf16[96,256]{1,0:T(8,128)(2,1)S(1)}, bf16[96,256]{1,0:T(8,128)(2,1)S(1)}, u32[]{:S(2)}, u32[]{:S(2)}) collective-permute-start(bf16[96,256]{1,0:T(8,128)(2,1)S(1)} %add_convert_fusion.2), channel_id=1, source_target_pairs={{0,3},{1,2},{2,1},{3,0},{4,7},{5,6},{6,5},{7,4},{8,11},{9,10},{10,... | collective-permute-start | bytes 147464 | tf_op jit(solution)/shard_map/ppermute | solution.py:400
  71.4 1.3 %collective-permute-start.27 = (bf16[96,256]{1,0:T(8,128)(2,1)S(1)}, bf16[96,256]{1,0:T(8,128)(2,1)S(1)}, u32[]{:S(2)}, u32[]{:S(2)}) collective-permute-start(bf16[96,256]{1,0:T(8,128)(2,1)S(1)} %add_convert_fusion.1.mine), channel_id=1, source_target_pairs={{0,4},{4,0},{8,12},{12,8},{16,20},{20,16},{24,28},{28,24},{1,5},{5... | collective-permute-start | bytes 147464 | tf_op jit(solution)/shard_map/ppermute | solution.py:400
where the time goes:
time: 74.2 us; the launch traced here: 74 us
  waiting for transfers between devices  32.1 us (43%)
  starting transfers between devices  26.3 us (35%)
  Pallas kernels  13.9 us (19%)
  between operations  1.5 us (2%)
    ppermute x28, waiting for transfers between devices, swap(): return lax.ppermute(value, axis, [(k, k ^ mask) for k in range(size)])  32.1 us
    ppermute x28, starting transfers between devices, swap(): return lax.ppermute(value, axis, [(k, k ^ mask) for k in range(size)])  26.3 us
    pallas_call x1, Pallas kernels, hidden_terms(): pl.pallas_call(functools.partial(hidden_kernel, n_row, n_col), out_shape=...  3.28 us
    pallas_call x1, Pallas kernels, gradients(): pl.pallas_call(functools.partial(gradient_kernel, n_col, classes), out_sh...  2.47 us
    pallas_call x1, Pallas kernels, first_near(): pl.pallas_call(functools.partial(first_near_kernel, n_row), out_shape=[ja...  2.12 us
    pallas_call x1, Pallas kernels, collect(): pl.pallas_call(functools.partial(collect_kernel, group, depth, tile_cols)...  1.93 us
    pallas_call x1, Pallas kernels, slopes(): pl.pallas_call(functools.partial(slope_kernel, n_row), out_shape=[jax.Sha...  1.49 us
  transfers between devices with their start and end apart: 28, of which 18 were waited for; matrix products, arithmetic and copies ran while one was open for 0% of the time, Pallas kernels for 7%

commit v1 on v0

--- a/solution.py
+++ b/solution.py
@@ -120,22 +120,7 @@
     return pl.ds(pl.multiple_of(position(row, k, n_row) * nodes, nodes), nodes)
 
 
-def stack(row, start, pieces, stacked):
-    nodes = pieces[0].shape[0]
-    for k, piece in enumerate(pieces):
-        place = pl.multiple_of(((row ^ (start + 2 * k)) >> 1) * nodes, nodes)
-        stacked[pl.ds(place, nodes), :] = piece[...]
-
-
-def parity_columns(parity, columns):
-    return pl.ds(pl.multiple_of(parity * (columns // 2), columns // 2), columns // 2)
-
-
-def first_near_kernel(n_row, ids, total, *refs):
-    pieces = refs[: n_row // 2]
-    dense, part, stacked = refs[n_row // 2 :]
-    row = ids[0]
-    stack(row, 0, pieces, stacked)
+def round_kernel(n_row, total, dense):
     tile_rows = dense.shape[0] // TILE
     tile_cols = dense.shape[1] // TILE
     each = tile_cols // n_row
@@ -148,66 +133,65 @@
             lanes = pl.ds(target * TILE, TILE)
             dense[lines, lanes] = total[tile_row * tile_cols + tile_col].astype(bf16)
 
-    part[...] = dot(dense[:, parity_columns(row & 1, dense.shape[1])], stacked[...])
-
-
-def first_near(ids, total, pieces, n_col):
-    nodes, width = pieces[0].shape
-    n_row = 2 * len(pieces)
-    size = (n_col * nodes, n_row * nodes)
-    return pl.pallas_call(
-        functools.partial(first_near_kernel, n_row),
-        out_shape=[jax.ShapeDtypeStruct(size, bf16), jax.ShapeDtypeStruct((size[0], width), f32)],
-        in_specs=[SMEM, VMEM] + [VMEM] * len(pieces),
-        out_specs=[VMEM] * 2,
-        scratch_shapes=[pltpu.VMEM((len(pieces) * nodes, width), bf16)],
-        compiler_params=params(size[0] * size[1] * 6 + 6 * MIB),
-        cost_estimate=cost(size[0] * size[1] * width, size[0] * size[1] * 6),
-        name="first_near",
-    )(ids, total, *pieces)
-
-
-def first_far_kernel(n_row, n_col, ids, dense, part, *refs):
-    pieces = refs[: n_row // 2]
-    outs, stacked = refs[n_row // 2 : -1], refs[-1]
-    nodes = pieces[0].shape[0]
-    row, col = ids[0], ids[1]
-    stack(row, 1, pieces, stacked)
-    columns = parity_columns(1 - (row & 1), dense.shape[1])
-    for k in range(n_col):
-        lines = pl.ds(pl.multiple_of((col ^ k) * nodes, nodes), nodes)
-        outs[k][...] = (part[lines, :] + dot(dense[lines, columns], stacked[...])).astype(bf16)
-
-
-def first_far(ids, dense, part, pieces, n_col):
-    nodes, width = pieces[0].shape
-    n_row = 2 * len(pieces)
-    return pl.pallas_call(
-        functools.partial(first_far_kernel, n_row, n_col),
-        out_shape=[jax.ShapeDtypeStruct((nodes, width), bf16)] * n_col,
-        in_specs=[SMEM, VMEM, VMEM] + [VMEM] * len(pieces),
-        out_specs=[VMEM] * n_col,
-        scratch_shapes=[pltpu.VMEM((len(pieces) * nodes, width), bf16)],
-        compiler_params=params(dense.size * 2 + 6 * MIB),
-        cost_estimate=cost(dense.size * width, dense.size),
-        name="first_far",
-    )(ids, dense, part, *pieces)
-
-
-def hidden_kernel(n_row, n_col, ids, dense, weight, bias, class_weight, code, *refs):
-    pieces = refs[:n_row]
-    hidden_out, column_out, term_out, stacked = refs[n_row:]
+
+def round_block(total, lines, columns, n_row):
+    return pl.pallas_call(
+        functools.partial(round_kernel, n_row),
+        out_shape=jax.ShapeDtypeStruct((lines, columns), bf16),
+        in_specs=[VMEM],
+        out_specs=VMEM,
+        compiler_params=params(lines * columns * 6 + 6 * MIB),
+        cost_estimate=cost(lines * columns, lines * columns * 6),
+        name="round_block",
+    )(total)
+
+
+def first_kernel(n_row, n_col, ids, dense, *refs):
+    pieces, outs = refs[:n_row], refs[n_row : n_row + n_col]
+    stacked, whole = refs[-2:]
     nodes = pieces[0].shape[0]
     row, col = ids[0], ids[1]
     for k in range(n_row):
-        pre = dot(pieces[k][...], weight[...]) + bias[...]
-        hidden = (pre * (1.0 / (1.0 + jnp.exp(-pre)))).astype(bf16)
-        place = place_of(row, k, n_row, nodes)
-        column_out[place, :] = hidden
-        if k == 0:
-            hidden_out[...] = hidden
+        stacked[place_of(row, k, n_row, nodes), :] = pieces[k][...]
+    whole[...] = dot(dense[...], stacked[...]).astype(bf16)
+    for k in range(n_col):
+        outs[k][...] = whole[pl.ds(pl.multiple_of((col ^ k) * nodes, nodes), nodes), :]
+
+
+def first_terms(ids, dense, pieces, n_col):
+    nodes, width = pieces[0].shape
+    n_row = len(pieces)
+    return pl.pallas_call(
+        functools.partial(first_kernel, n_row, n_col),
+        out_shape=[jax.ShapeDtypeStruct((nodes, width), bf16)] * n_col,
+        in_specs=[SMEM, VMEM] + [VMEM] * n_row,
+        out_specs=[VMEM] * n_col,
+        scratch_shapes=[
+            pltpu.VMEM((n_row * nodes, width), bf16),
+            pltpu.VMEM((n_col * nodes, width), bf16),
+        ],
+        compiler_params=params(dense.size * 2 + 6 * MIB),
+        cost_estimate=cost(2 * dense.size * width, dense.size * 2),
+        name="first_terms",
+    )(ids, dense, *pieces)
+
+
+def hidden_kernel(n_row, n_col, ids, dense, weight, bias, class_weight, code, *refs):
+    pieces = refs[:n_row]
+    hidden_out, column_out, term_out, stacked, gathered = refs[n_row:]
+    nodes = pieces[0].shape[0]
+    row, col = ids[0], ids[1]
+    for k in range(n_row):
+        gathered[place_of(row, k, n_row, nodes), :] = pieces[k][...]
+    chunk = 2 * nodes
+    for k in range(n_row // 2):
+        lines = pl.ds(k * chunk, chunk)
+        pre = dot(gathered[lines, :], weight[...]) + bias[...]
+        hidden = (pre / (1.0 + jnp.exp(-pre))).astype(bf16)
+        column_out[lines, :] = hidden
         high, low = halves(dot(hidden, class_weight[...], ((1,), (1,))))
-        stacked[place, :] = jnp.concatenate([high, low], axis=1)
+        stacked[lines, :] = jnp.concatenate([high, low], axis=1)
+    hidden_out[...] = column_out[place_of(row, 0, n_row, nodes), :]
     both = dot(dense[...], stacked[...])
     lanes = both.shape[1] // 2
     term = (both[:, :lanes] + both[:, lanes:]).T[: term_out.shape[0]]
@@ -232,7 +216,10 @@
         ],
         in_specs=[SMEM] + [VMEM] * (5 + n_row),
         out_specs=[VMEM] * 3,
-        scratch_shapes=[pltpu.VMEM((column, 2 * lanes), bf16)],
+        scratch_shapes=[
+            pltpu.VMEM((column, 2 * lanes), bf16),
+            pltpu.VMEM((column, pieces[0].shape[1]), bf16),
+        ],
         compiler_params=params(dense.size * 2 + column * width * 8 + 6 * MIB),
         cost_estimate=cost(4 * dense.size * lanes, dense.size * 2, column * width * 2),
         name="hidden_terms",
@@ -446,8 +433,8 @@
     total = collect(
         tile_values[0, 0], tile_rows[0], tile_cols[0], tile_count, n_col * nodes // TILE, n_row * nodes // TILE
     )
-    dense, part = first_near(ids, total, near, n_col)
-    terms = first_far(ids, dense, part, far, n_col)
+    dense = round_block(total, n_col * nodes, n_row * nodes, n_row)
+    terms = first_terms(ids, dense, [piece for pair in zip(near, far) for piece in pair], n_col)
     arrived = [terms[0]] + [swap(terms[k], "col", k) for k in range(1, n_col)]
     first_agg = tree_sum(arrived).astype(bf16)
     near, far = gather_row(first_agg)

time: 74.2 us -> 70.5 us (0.950)
  waiting for transfers between devices: 32.1 us -> 28.2 us
  starting transfers between devices: 26.3 us -> 27.9 us
  Pallas kernels: 13.9 us -> 12.5 us
    ppermute x28, waiting for transfers between devices: 32.1 us -> 28.2 us  [swap(): return lax.ppermute(value, axis, [(k, k ^ mask) for k in range(size)])]
    ppermute x28, starting transfers between devices: 26.3 us -> 27.9 us  [swap(): return lax.ppermute(value, axis, [(k, k ^ mask) for k in range(size)])]
  transfers between devices with their start and end apart: 28 -> 28, of which waited for: 18 -> 18; matrix products, arithmetic and copies ran while one was open for 0% -> 0% of each run, Pallas kernels for 7% -> 6%
where the time goes in v1:
time: 70.5 us; the launch traced here: 70.4 us
  waiting for transfers between devices  28.2 us (40%)
  starting transfers between devices  27.9 us (40%)
  Pallas kernels  12.5 us (18%)
  between operations  1.51 us (2%)
    ppermute x28, waiting for transfers between devices, swap(): return lax.ppermute(value, axis, [(k, k ^ mask) for k in range(size)])  28.2 us
    ppermute x28, starting transfers between devices, swap(): return lax.ppermute(value, axis, [(k, k ^ mask) for k in range(size)])  27.9 us
    pallas_call x1, Pallas kernels, hidden_terms(): pl.pallas_call(functools.partial(hidden_kernel, n_row, n_col), out_shape=...  2.6 us
    pallas_call x1, Pallas kernels, gradients(): pl.pallas_call(functools.partial(gradient_kernel, n_col, classes), out_sh...  2.45 us
    pallas_call x1, Pallas kernels, collect(): pl.pallas_call(functools.partial(collect_kernel, group, depth, tile_cols)...  1.9 us
    pallas_call x1, Pallas kernels, first_terms(): pl.pallas_call(functools.partial(first_kernel, n_row, n_col), out_shape=[...  1.85 us
    pallas_call x1, Pallas kernels, slopes(): pl.pallas_call(functools.partial(slope_kernel, n_row), out_shape=[jax.Sha...  1.49 us
  transfers between devices with their start and end apart: 28, of which 18 were waited for; matrix products, arithmetic and copies ran while one was open for 0% of the time, Pallas kernels for 6%

profile of v1, /device:TPU:0, one launch (start us, length us, event | category | flops | bytes accessed | tf_op | source)
XLA Modules:
  0.0 70.4 jit_solution(2704688638191276398)
XLA Ops:
  0.6 3.0 %collective-permute-start.1 = (bf16[256,128]{1,0:T(8,128)(2,1)}, bf16[256,128]{1,0:T(8,128)(2,1)S(1)}, u32[]{:S(2)}, u32[]{:S(2)}) collective-permute-start(bf16[256,128]{1,0:T(8,128)(2,1)} %refs_0_.1), channel_id=1, source_target_pairs={{0,8},{4,12},{8,0},{12,4},{16,24},{20,28},{24,16},{28,20},{1,9},{5... | collective-permute-start | bytes 196616 | tf_op jit(solution)/shard_map/ppermute | solution.py:387
  3.7 1.5 %collective-permute-start.3 = (bf16[256,128]{1,0:T(8,128)(2,1)}, bf16[256,128]{1,0:T(8,128)(2,1)S(1)}, u32[]{:S(2)}, u32[]{:S(2)}) collective-permute-start(bf16[256,128]{1,0:T(8,128)(2,1)} %refs_0_.1), channel_id=1, source_target_pairs={{0,16},{4,20},{8,24},{12,28},{16,0},{20,4},{24,8},{28,12},{1,17},{... | collective-permute-start | bytes 196616 | tf_op jit(solution)/shard_map/ppermute | solution.py:387
  5.2 0.0 collective-permute-start.5
  5.9 1.9 %collect.1.total = f32[129,128,128]{2,1,0:T(8,128)S(1)} custom-call(s32[1,1]{1,0:T(1,128)S(6)} %copy.18.count, s32[1,384]{1,0:T(1,128)} %bitcast.19, s32[1,384]{1,0:T(1,128)} %bitcast.20, bf16[384,128,128]{2,1,0:T(8,128)(2,1)} %bitcast.17), custom_call_target="tpu_custom_call" | custom-call | flops 6291456 | bytes 12582912 | tf_op jit(solution)/shard_map/collect/pallas_call | solution.py:96
  7.8 0.0 copy-start.4
  7.9 0.8 %round_block.1.dense = bf16[1024,2048]{1,0:T(8,128)(2,1)S(1)} custom-call(f32[129,128,128]{2,1,0:T(8,128)S(1)} %collect.1.total), custom_call_target="tpu_custom_call" | custom-call | flops 2097152 | bytes 12582912 | tf_op jit(solution)/shard_map/round_block/pallas_call | solution.py:138
  8.7 1.2 %collective-permute-start.2 = (bf16[256,128]{1,0:T(8,128)(2,1)S(1)}, bf16[256,128]{1,0:T(8,128)(2,1)S(1)}, u32[]{:S(2)}, u32[]{:S(2)}) collective-permute-start(bf16[256,128]{1,0:T(8,128)(2,1)S(1)} %collective-permute-done.1.refs_2_), channel_id=1, source_target_pairs={{0,4},{4,0},{8,12},{12,8},{16,20},{20,16},{24,28},{28,24},{1,5},{5... | collective-permute-start | bytes 196616 | tf_op jit(solution)/shard_map/ppermute | solution.py:387
  9.9 0.1 collective-permute-start.4
  10.0 0.6 collective-permute-done.5.refs_6_
  10.6 0.1 pad_add_fusion.ids
  10.6 0.2 collective-permute-done.2.refs_3_
  10.8 0.4 collective-permute-done.4.refs_5_
  11.2 0.6 collective-permute-done.6.refs_7_
  11.8 1.8 %first_terms.1 = (bf16[256,128]{1,0:T(8,128)(2,1)S(1)}, bf16[256,128]{1,0:T(8,128)(2,1)S(1)}, bf16[256,128]{1,0:T(8,128)(2,1)S(1)}, bf16[256,128]{1,0:T(8,128)(2,1)S(1)}) custom-call(s32[2]{0:T(128)S(1)} %pad_add_fusion.ids, bf16[1024,2048]{1,0:T(8,128)(2,1)S(1)} %round_block.1.dense, bf16[256,128]{1,0:T(8,128)(2,1)S(1)} %copy-done, ...), custom_call_target="tpu_custom_call" | custom-call | flops 536870912 | bytes 4194304 | tf_op jit(solution)/shard_map/first_terms/pallas_call | solution.py:164
  13.7 1.6 %collective-permute-start.7 = (bf16[256,128]{1,0:T(8,128)(2,1)S(1)}, bf16[256,128]{1,0:T(8,128)(2,1)S(1)}, u32[]{:S(2)}, u32[]{:S(2)}) collective-permute-start(bf16[256,128]{1,0:T(8,128)(2,1)S(1)} %get-tuple-element.25), channel_id=1, source_target_pairs={{0,1},{1,0},{2,3},{3,2},{4,5},{5,4},{6,7},{7,6},{8,9},{9,8},{10,11... | collective-permute-start | bytes 196616 | tf_op jit(solution)/shard_map/ppermute | solution.py:387
  15.3 2.9 %collective-permute-start.8 = (bf16[256,128]{1,0:T(8,128)(2,1)S(1)}, bf16[256,128]{1,0:T(8,128)(2,1)S(1)}, u32[]{:S(2)}, u32[]{:S(2)}) collective-permute-start(bf16[256,128]{1,0:T(8,128)(2,1)S(1)} %get-tuple-element.26), channel_id=1, source_target_pairs={{0,2},{1,3},{2,0},{3,1},{4,6},{5,7},{6,4},{7,5},{8,10},{9,11},{10,... | collective-permute-start | bytes 196616 | tf_op jit(solution)/shard_map/ppermute | solution.py:387
  18.2 4.2 %collective-permute-done.8 = bf16[256,128]{1,0:T(8,128)(2,1)S(1)} collective-permute-done((bf16[256,128]{1,0:T(8,128)(2,1)S(1)}, bf16[256,128]{1,0:T(8,128)(2,1)S(1)}, u32[]{:S(2)}, u32[]{:S(2)}) %collective-permute-start.8) | collective-permute-done | bytes 65568 | tf_op jit(solution)/shard_map/ppermute | solution.py:387
  22.4 1.9 %collective-permute-done.9 = bf16[256,128]{1,0:T(8,128)(2,1)S(1)} collective-permute-done((bf16[256,128]{1,0:T(8,128)(2,1)S(1)}, bf16[256,128]{1,0:T(8,128)(2,1)S(1)}, u32[]{:S(2)}, u32[]{:S(2)}) %collective-permute-start.9) | collective-permute-done | bytes 65568 | tf_op jit(solution)/shard_map/ppermute | solution.py:387
  24.3 1.5 %collective-permute-start.11 = (bf16[256,128]{1,0:T(8,128)(2,1)S(1)}, bf16[256,128]{1,0:T(8,128)(2,1)S(1)}, u32[]{:S(2)}, u32[]{:S(2)}) collective-permute-start(bf16[256,128]{1,0:T(8,128)(2,1)S(1)} %add_convert_fusion.refs_0_), channel_id=1, source_target_pairs={{0,8},{4,12},{8,0},{12,4},{16,24},{20,28},{24,16},{28,20},{1,9},{5... | collective-permute-start | bytes 196616 | tf_op jit(solution)/shard_map/ppermute | solution.py:387
  25.8 1.7 %collective-permute-start.13 = (bf16[256,128]{1,0:T(8,128)(2,1)S(1)}, bf16[256,128]{1,0:T(8,128)(2,1)S(1)}, u32[]{:S(2)}, u32[]{:S(2)}) collective-permute-start(bf16[256,128]{1,0:T(8,128)(2,1)S(1)} %add_convert_fusion.refs_0_), channel_id=1, source_target_pairs={{0,16},{4,20},{8,24},{12,28},{16,0},{20,4},{24,8},{28,12},{1,17},{... | collective-permute-start | bytes 196616 | tf_op jit(solution)/shard_map/ppermute | solution.py:387
  27.5 0.9 %collective-permute-start.15 = (bf16[256,128]{1,0:T(8,128)(2,1)S(1)}, bf16[256,128]{1,0:T(8,128)(2,1)S(1)}, u32[]{:S(2)}, u32[]{:S(2)}) collective-permute-start(bf16[256,128]{1,0:T(8,128)(2,1)S(1)} %add_convert_fusion.refs_0_), channel_id=1, source_target_pairs={{0,24},{4,28},{8,16},{12,20},{16,8},{20,12},{24,0},{28,4},{1,25},{... | collective-permute-start | bytes 196616 | tf_op jit(solution)/shard_map/ppermute | solution.py:387
  28.5 0.2 collective-permute-done.11.refs_2_
  28.6 0.3 collective-permute-start.12
  29.0 1.1 %collective-permute-done.13.refs_4_ = bf16[256,128]{1,0:T(8,128)(2,1)S(1)} collective-permute-done((bf16[256,128]{1,0:T(8,128)(2,1)S(1)}, bf16[256,128]{1,0:T(8,128)(2,1)S(1)}, u32[]{:S(2)}, u32[]{:S(2)}) %collective-permute-start.13) | collective-permute-done | bytes 65568 | tf_op jit(solution)/shard_map/ppermute | solution.py:387
  30.1 2.6 %collective-permute-done.15.refs_6_ = bf16[256,128]{1,0:T(8,128)(2,1)S(1)} collective-permute-done((bf16[256,128]{1,0:T(8,128)(2,1)S(1)}, bf16[256,128]{1,0:T(8,128)(2,1)S(1)}, u32[]{:S(2)}, u32[]{:S(2)}) %collective-permute-start.15) | collective-permute-done | bytes 65568 | tf_op jit(solution)/shard_map/ppermute | solution.py:387
  32.8 1.2 %collective-permute-done.16.refs_7_ = bf16[256,128]{1,0:T(8,128)(2,1)S(1)} collective-permute-done((bf16[256,128]{1,0:T(8,128)(2,1)S(1)}, bf16[256,128]{1,0:T(8,128)(2,1)S(1)}, u32[]{:S(2)}, u32[]{:S(2)}) %collective-permute-start.16) | collective-permute-done | bytes 65568 | tf_op jit(solution)/shard_map/ppermute | solution.py:387
  34.0 2.6 %hidden_terms.1 = (bf16[256,256]{1,0:T(8,128)(2,1)}, bf16[2048,256]{1,0:T(8,128)(2,1)S(1)}, bf16[48,1024]{1,0:T(8,128)(2,1)S(1)}) custom-call(s32[2]{0:T(128)S(1)} %pad_add_fusion.ids, bf16[1024,2048]{1,0:T(8,128)(2,1)S(1)} %round_block.1.dense, bf16[128,256]{1,0:T(8,128)(2,1)S(1)} %copy-done.1, f32[1,256]{1,0:T(1,128)S(1)} %bitcast.15, ...), custom_call_target="tpu_custom_call" | custom-call | flops 1073741824 | bytes 4194304 | tf_op jit(solution)/shard_map/hidden_terms/pallas_call | solution.py:210
  36.6 1.5 %collective-permute-start.17 = (bf16[48,1024]{1,0:T(8,128)(2,1)S(1)}, bf16[48,1024]{1,0:T(8,128)(2,1)S(1)}, u32[]{:S(2)}, u32[]{:S(2)}) collective-permute-start(bf16[48,1024]{1,0:T(8,128)(2,1)S(1)} %get-tuple-element.32.refs_0_), channel_id=1, source_target_pairs={{0,1},{1,0},{2,3},{3,2},{4,5},{5,4},{6,7},{7,6},{8,9},{9,8},{10,11... | collective-permute-start | bytes 294920 | tf_op jit(solution)/shard_map/ppermute | solution.py:387
  38.0 1.4 %collective-permute-start.18 = (bf16[48,1024]{1,0:T(8,128)(2,1)S(1)}, bf16[48,1024]{1,0:T(8,128)(2,1)S(1)}, u32[]{:S(2)}, u32[]{:S(2)}) collective-permute-start(bf16[48,1024]{1,0:T(8,128)(2,1)S(1)} %get-tuple-element.32.refs_0_), channel_id=1, source_target_pairs={{0,2},{1,3},{2,0},{3,1},{4,6},{5,7},{6,4},{7,5},{8,10},{9,11},{10,... | collective-permute-start | bytes 294920 | tf_op jit(solution)/shard_map/ppermute | solution.py:387
  39.4 1.6 %collective-permute-start.19 = (bf16[48,1024]{1,0:T(8,128)(2,1)S(1)}, bf16[48,1024]{1,0:T(8,128)(2,1)S(1)}, u32[]{:S(2)}, u32[]{:S(2)}) collective-permute-start(bf16[48,1024]{1,0:T(8,128)(2,1)S(1)} %get-tuple-element.32.refs_0_), channel_id=1, source_target_pairs={{0,3},{1,2},{2,1},{3,0},{4,7},{5,6},{6,5},{7,4},{8,11},{9,10},{10,... | collective-permute-start | bytes 294920 | tf_op jit(solution)/shard_map/ppermute | solution.py:387
  41.0 1.5 %slopes.1 = (f32[2048,256]{1,0:T(8,128)S(1)}, bf16[128,2048]{1,0:T(8,128)(2,1)S(1)}) custom-call(s32[2]{0:T(128)S(1)} %pad_add_fusion.ids, bf16[128,256]{1,0:T(8,128)(2,1)S(1)} %copy-done.1, f32[1,256]{1,0:T(1,128)S(1)} %bitcast.16, bf16[256,128]{1,0:T(8,128)(2,1)S(1)} %add_convert_fusion.refs_0_, bf16[256,128]{1,0:T(8,128)(2,1)S(1)} %collective-permute-done.10.refs_1_, ...), custom_call_target="tpu_custom_call" | custom-call | flops 134217728 | bytes 2097152 | tf_op jit(solution)/shard_map/slopes/pallas_call | solution.py:247
  42.5 6.1 %collective-permute-done.18.refs_2_ = bf16[48,1024]{1,0:T(8,128)(2,1)S(1)} collective-permute-done((bf16[48,1024]{1,0:T(8,128)(2,1)S(1)}, bf16[48,1024]{1,0:T(8,128)(2,1)S(1)}, u32[]{:S(2)}, u32[]{:S(2)}) %collective-permute-start.18) | collective-permute-done | bytes 98336 | tf_op jit(solution)/shard_map/ppermute | solution.py:387
  48.6 2.5 %gradients.1 = (f32[47,256]{1,0:T(8,128)}, bf16[96,256]{1,0:T(8,128)(2,1)S(1)}, bf16[96,256]{1,0:T(8,128)(2,1)S(1)}) custom-call(s32[2]{0:T(128)S(1)} %pad_add_fusion.ids, bf16[1024,2048]{1,0:T(8,128)(2,1)S(1)} %round_block.1.dense, bf16[2048,256]{1,0:T(8,128)(2,1)S(1)} %get-tuple-element.29.column, f32[2048,256]{1,0:T(8,128)S(1)} %get-tuple-element.30.slope, ...), custom_call_target="tpu_custom_call" | custom-call | flops 402653184 | bytes 4194304 | tf_op jit(solution)/shard_map/gradients/pallas_call | solution.py:332
  51.1 0.1 collective-permute-start.20
  51.2 1.2 %collective-permute-done.20 = bf16[96,256]{1,0:T(8,128)(2,1)S(1)} collective-permute-done((bf16[96,256]{1,0:T(8,128)(2,1)S(1)}, bf16[96,256]{1,0:T(8,128)(2,1)S(1)}, u32[]{:S(2)}, u32[]{:S(2)}) %collective-permute-start.20) | collective-permute-done | bytes 49184 | tf_op jit(solution)/shard_map/ppermute | solution.py:387
  52.4 1.5 %collective-permute-start.21 = (bf16[96,256]{1,0:T(8,128)(2,1)S(1)}, bf16[96,256]{1,0:T(8,128)(2,1)S(1)}, u32[]{:S(2)}, u32[]{:S(2)}) collective-permute-start(bf16[96,256]{1,0:T(8,128)(2,1)S(1)} %add_convert_fusion.3), channel_id=1, source_target_pairs={{0,8},{4,12},{8,0},{12,4},{16,24},{20,28},{24,16},{28,20},{1,9},{5... | collective-permute-start | bytes 147464 | tf_op jit(solution)/shard_map/ppermute | solution.py:387
  54.0 0.2 collective-permute-start.22
  54.2 1.8 %collective-permute-start.23 = (bf16[96,256]{1,0:T(8,128)(2,1)S(1)}, bf16[96,256]{1,0:T(8,128)(2,1)S(1)}, u32[]{:S(2)}, u32[]{:S(2)}) collective-permute-start(bf16[96,256]{1,0:T(8,128)(2,1)S(1)} %add_convert_fusion.3), channel_id=1, source_target_pairs={{0,24},{4,28},{8,16},{12,20},{16,8},{20,12},{24,0},{28,4},{1,25},{... | collective-permute-start | bytes 147464 | tf_op jit(solution)/shard_map/ppermute | solution.py:387
  56.0 0.6 collective-permute-done.21
  56.6 1.8 %collective-permute-done.22 = bf16[96,256]{1,0:T(8,128)(2,1)S(1)} collective-permute-done((bf16[96,256]{1,0:T(8,128)(2,1)S(1)}, bf16[96,256]{1,0:T(8,128)(2,1)S(1)}, u32[]{:S(2)}, u32[]{:S(2)}) %collective-permute-start.22) | collective-permute-done | bytes 49184 | tf_op jit(solution)/shard_map/ppermute | solution.py:387
  58.4 0.8 %collective-permute-done.23 = bf16[96,256]{1,0:T(8,128)(2,1)S(1)} collective-permute-done((bf16[96,256]{1,0:T(8,128)(2,1)S(1)}, bf16[96,256]{1,0:T(8,128)(2,1)S(1)}, u32[]{:S(2)}, u32[]{:S(2)}) %collective-permute-start.23) | collective-permute-done | bytes 49184 | tf_op jit(solution)/shard_map/ppermute | solution.py:387
  59.2 2.5 %collective-permute-start.24 = (bf16[96,256]{1,0:T(8,128)(2,1)S(1)}, bf16[96,256]{1,0:T(8,128)(2,1)S(1)}, u32[]{:S(2)}, u32[]{:S(2)}) collective-permute-start(bf16[96,256]{1,0:T(8,128)(2,1)S(1)} %add_convert_fusion.2), channel_id=1, source_target_pairs={{0,1},{1,0},{2,3},{3,2},{4,5},{5,4},{6,7},{7,6},{8,9},{9,8},{10,11... | collective-permute-start | bytes 147464 | tf_op jit(solution)/shard_map/ppermute | solution.py:387
  61.7 2.4 %collective-permute-start.26 = (bf16[96,256]{1,0:T(8,128)(2,1)S(1)}, bf16[96,256]{1,0:T(8,128)(2,1)S(1)}, u32[]{:S(2)}, u32[]{:S(2)}) collective-permute-start(bf16[96,256]{1,0:T(8,128)(2,1)S(1)} %add_convert_fusion.2), channel_id=1, source_target_pairs={{0,3},{1,2},{2,1},{3,0},{4,7},{5,6},{6,5},{7,4},{8,11},{9,10},{10,... | collective-permute-start | bytes 147464 | tf_op jit(solution)/shard_map/ppermute | solution.py:387
  64.2 2.6 %collective-permute-done.25 = bf16[96,256]{1,0:T(8,128)(2,1)S(1)} collective-permute-done((bf16[96,256]{1,0:T(8,128)(2,1)S(1)}, bf16[96,256]{1,0:T(8,128)(2,1)S(1)}, u32[]{:S(2)}, u32[]{:S(2)}) %collective-permute-start.25) | collective-permute-done | bytes 49184 | tf_op jit(solution)/shard_map/ppermute | solution.py:387
  66.7 1.0 %collective-permute-done.26 = bf16[96,256]{1,0:T(8,128)(2,1)S(1)} collective-permute-done((bf16[96,256]{1,0:T(8,128)(2,1)S(1)}, bf16[96,256]{1,0:T(8,128)(2,1)S(1)}, u32[]{:S(2)}, u32[]{:S(2)}) %collective-permute-start.26) | collective-permute-done | bytes 49184 | tf_op jit(solution)/shard_map/ppermute | solution.py:387
  67.7 0.1 collective-permute-start.27
  67.8 1.2 %collective-permute-done.27.other = bf16[96,256]{1,0:T(8,128)(2,1)S(1)} collective-permute-done((bf16[96,256]{1,0:T(8,128)(2,1)S(1)}, bf16[96,256]{1,0:T(8,128)(2,1)S(1)}, u32[]{:S(2)}, u32[]{:S(2)}) %collective-permute-start.27) | collective-permute-done | bytes 49184 | tf_op jit(solution)/shard_map/ppermute | solution.py:387
  69.0 1.3 %finish.1 = (f32[1,1]{1,0:T(1,128)}, f32[128,256]{1,0:T(8,128)}, f32[1,256]{1,0:T(1,128)}, f32[47,256]{1,0:T(8,128)}, f32[1,47]{1,0:T(1,128)}) custom-call(s32[2]{0:T(128)S(1)} %pad_add_fusion.ids, bf16[96,256]{1,0:T(8,128)(2,1)S(1)} %add_convert_fusion.1.mine, bf16[96,256]{1,0:T(8,128)(2,1)S(1)} %collective-permute-done.27.other), custom_call_target="tpu_custom_call" | custom-call | tf_op jit(solution)/shard_map/finish/pallas_call | solution.py:368
  (37 shorter events, 0.2 us)
Async XLA Ops:
  0.6 8.1 %collective-permute-start.1 = (bf16[256,128]{1,0:T(8,128)(2,1)}, bf16[256,128]{1,0:T(8,128)(2,1)S(1)}, u32[]{:S(2)}, u32[]{:S(2)}) collective-permute-start(bf16[256,128]{1,0:T(8,128)(2,1)} %refs_0_.1), channel_id=1, source_target_pairs={{0,8},{4,12},{8,0},{12,4},{16,24},{20,28},{24,16},{28,20},{1,9},{5... | collective-permute-start | bytes 196616 | tf_op jit(solution)/shard_map/ppermute | solution.py:387
  3.7 6.2 %collective-permute-start.3 = (bf16[256,128]{1,0:T(8,128)(2,1)}, bf16[256,128]{1,0:T(8,128)(2,1)S(1)}, u32[]{:S(2)}, u32[]{:S(2)}) collective-permute-start(bf16[256,128]{1,0:T(8,128)(2,1)} %refs_0_.1), channel_id=1, source_target_pairs={{0,16},{4,20},{8,24},{12,28},{16,0},{20,4},{24,8},{28,12},{1,17},{... | collective-permute-start | bytes 196616 | tf_op jit(solution)/shard_map/ppermute | solution.py:387
  5.2 5.4 %collective-permute-start.5 = (bf16[256,128]{1,0:T(8,128)(2,1)}, bf16[256,128]{1,0:T(8,128)(2,1)S(1)}, u32[]{:S(2)}, u32[]{:S(2)}) collective-permute-start(bf16[256,128]{1,0:T(8,128)(2,1)} %refs_0_.1), channel_id=1, source_target_pairs={{0,24},{4,28},{8,16},{12,20},{16,8},{20,12},{24,0},{28,4},{1,25},{... | collective-permute-start | bytes 196616 | tf_op jit(solution)/shard_map/ppermute | solution.py:387
  5.2 5.4 %collective-permute-start = (bf16[256,128]{1,0:T(8,128)(2,1)}, bf16[256,128]{1,0:T(8,128)(2,1)S(1)}, u32[]{:S(2)}, u32[]{:S(2)}) collective-permute-start(bf16[256,128]{1,0:T(8,128)(2,1)} %refs_0_.1), channel_id=1, source_target_pairs={{0,4},{4,0},{8,12},{12,8},{16,20},{20,16},{24,28},{28,24},{1,5},{5... | collective-permute-start | bytes 196616 | tf_op jit(solution)/shard_map/ppermute | solution.py:387
  7.8 4.0 %copy-start = (bf16[256,128]{1,0:T(8,128)(2,1)S(1)}, bf16[256,128]{1,0:T(8,128)(2,1)}, u32[]{:S(2)}) copy-start(bf16[256,128]{1,0:T(8,128)(2,1)} %refs_0_.1) | copy-start | bytes 196612
  7.8 24.9 %copy-start.4 = (s32[256]{0:T(256)S(1)}, s32[256]{0:T(256)}, u32[]{:S(2)}) copy-start(s32[256]{0:T(256)} %param.16) | copy-start | bytes 3076
  7.8 24.9 %copy-start.5 = (s32[256]{0:T(256)S(1)}, s32[256]{0:T(256)}, u32[]{:S(2)}) copy-start(s32[256]{0:T(256)} %param.17) | copy-start | bytes 3076
  7.8 24.9 %copy-start.3 = (bf16[256,47]{0,1:T(8,128)(2,1)S(1)}, bf16[256,47]{0,1:T(8,128)(2,1)}, u32[]{:S(2)}) copy-start(bf16[256,47]{0,1:T(8,128)(2,1)} %param.20) | copy-start | bytes 72196
  7.8 26.1 %copy-start.1 = (bf16[128,256]{1,0:T(8,128)(2,1)S(1)}, bf16[128,256]{1,0:T(8,128)(2,1)}, u32[]{:S(2)}) copy-start(bf16[128,256]{1,0:T(8,128)(2,1)} %weight.3) | copy-start | bytes 196612
  7.8 26.1 %copy-start.2 = (f32[256]{0:T(256)S(1)}, f32[256]{0:T(256)}, u32[]{:S(2)}) copy-start(f32[256]{0:T(256)} %param.19) | copy-start | bytes 3076
  7.8 33.2 %copy-start.6 = (f32[47]{0:T(128)S(1)}, f32[47]{0:T(128)}, u32[]{:S(2)}) copy-start(f32[47]{0:T(128)} %param.21) | copy-start | bytes 568
  8.7 2.1 %collective-permute-start.2 = (bf16[256,128]{1,0:T(8,128)(2,1)S(1)}, bf16[256,128]{1,0:T(8,128)(2,1)S(1)}, u32[]{:S(2)}, u32[]{:S(2)}) collective-permute-start(bf16[256,128]{1,0:T(8,128)(2,1)S(1)} %collective-permute-done.1.refs_2_), channel_id=1, source_target_pairs={{0,4},{4,0},{8,12},{12,8},{16,20},{20,16},{24,28},{28,24},{1,5},{5... | collective-permute-start | bytes 196616 | tf_op jit(solution)/shard_map/ppermute | solution.py:387
  9.9 1.3 %collective-permute-start.4 = (bf16[256,128]{1,0:T(8,128)(2,1)S(1)}, bf16[256,128]{1,0:T(8,128)(2,1)S(1)}, u32[]{:S(2)}, u32[]{:S(2)}) collective-permute-start(bf16[256,128]{1,0:T(8,128)(2,1)S(1)} %collective-permute-done.3.refs_4_), channel_id=1, source_target_pairs={{0,4},{4,0},{8,12},{12,8},{16,20},{20,16},{24,28},{28,24},{1,5},{5... | collective-permute-start | bytes 196616 | tf_op jit(solution)/shard_map/ppermute | solution.py:387
  10.6 1.3 %collective-permute-start.6 = (bf16[256,128]{1,0:T(8,128)(2,1)S(1)}, bf16[256,128]{1,0:T(8,128)(2,1)S(1)}, u32[]{:S(2)}, u32[]{:S(2)}) collective-permute-start(bf16[256,128]{1,0:T(8,128)(2,1)S(1)} %collective-permute-done.5.refs_6_), channel_id=1, source_target_pairs={{0,4},{4,0},{8,12},{12,8},{16,20},{20,16},{24,28},{28,24},{1,5},{5... | collective-permute-start | bytes 196616 | tf_op jit(solution)/shard_map/ppermute | solution.py:387
  13.7 4.5 %collective-permute-start.7 = (bf16[256,128]{1,0:T(8,128)(2,1)S(1)}, bf16[256,128]{1,0:T(8,128)(2,1)S(1)}, u32[]{:S(2)}, u32[]{:S(2)}) collective-permute-start(bf16[256,128]{1,0:T(8,128)(2,1)S(1)} %get-tuple-element.25), channel_id=1, source_target_pairs={{0,1},{1,0},{2,3},{3,2},{4,5},{5,4},{6,7},{7,6},{8,9},{9,8},{10,11... | collective-permute-start | bytes 196616 | tf_op jit(solution)/shard_map/ppermute | solution.py:387
  15.3 7.1 %collective-permute-start.8 = (bf16[256,128]{1,0:T(8,128)(2,1)S(1)}, bf16[256,128]{1,0:T(8,128)(2,1)S(1)}, u32[]{:S(2)}, u32[]{:S(2)}) collective-permute-start(bf16[256,128]{1,0:T(8,128)(2,1)S(1)} %get-tuple-element.26), channel_id=1, source_target_pairs={{0,2},{1,3},{2,0},{3,1},{4,6},{5,7},{6,4},{7,5},{8,10},{9,11},{10,... | collective-permute-start | bytes 196616 | tf_op jit(solution)/shard_map/ppermute | solution.py:387
  18.2 6.1 %collective-permute-start.9 = (bf16[256,128]{1,0:T(8,128)(2,1)S(1)}, bf16[256,128]{1,0:T(8,128)(2,1)S(1)}, u32[]{:S(2)}, u32[]{:S(2)}) collective-permute-start(bf16[256,128]{1,0:T(8,128)(2,1)S(1)} %get-tuple-element.27), channel_id=1, source_target_pairs={{0,3},{1,2},{2,1},{3,0},{4,7},{5,6},{6,5},{7,4},{8,11},{9,10},{10,... | collective-permute-start | bytes 196616 | tf_op jit(solution)/shard_map/ppermute | solution.py:387
  24.3 4.3 %collective-permute-start.11 = (bf16[256,128]{1,0:T(8,128)(2,1)S(1)}, bf16[256,128]{1,0:T(8,128)(2,1)S(1)}, u32[]{:S(2)}, u32[]{:S(2)}) collective-permute-start(bf16[256,128]{1,0:T(8,128)(2,1)S(1)} %add_convert_fusion.refs_0_), channel_id=1, source_target_pairs={{0,8},{4,12},{8,0},{12,4},{16,24},{20,28},{24,16},{28,20},{1,9},{5... | collective-permute-start | bytes 196616 | tf_op jit(solution)/shard_map/ppermute | solution.py:387
  25.8 4.3 %collective-permute-start.13 = (bf16[256,128]{1,0:T(8,128)(2,1)S(1)}, bf16[256,128]{1,0:T(8,128)(2,1)S(1)}, u32[]{:S(2)}, u32[]{:S(2)}) collective-permute-start(bf16[256,128]{1,0:T(8,128)(2,1)S(1)} %add_convert_fusion.refs_0_), channel_id=1, source_target_pairs={{0,16},{4,20},{8,24},{12,28},{16,0},{20,4},{24,8},{28,12},{1,17},{... | collective-permute-start | bytes 196616 | tf_op jit(solution)/shard_map/ppermute | solution.py:387
  27.5 5.2 %collective-permute-start.15 = (bf16[256,128]{1,0:T(8,128)(2,1)S(1)}, bf16[256,128]{1,0:T(8,128)(2,1)S(1)}, u32[]{:S(2)}, u32[]{:S(2)}) collective-permute-start(bf16[256,128]{1,0:T(8,128)(2,1)S(1)} %add_convert_fusion.refs_0_), channel_id=1, source_target_pairs={{0,24},{4,28},{8,16},{12,20},{16,8},{20,12},{24,0},{28,4},{1,25},{... | collective-permute-start | bytes 196616 | tf_op jit(solution)/shard_map/ppermute | solution.py:387
  28.5 4.3 %collective-permute-start.10 = (bf16[256,128]{1,0:T(8,128)(2,1)S(1)}, bf16[256,128]{1,0:T(8,128)(2,1)S(1)}, u32[]{:S(2)}, u32[]{:S(2)}) collective-permute-start(bf16[256,128]{1,0:T(8,128)(2,1)S(1)} %add_convert_fusion.refs_0_), channel_id=1, source_target_pairs={{0,4},{4,0},{8,12},{12,8},{16,20},{20,16},{24,28},{28,24},{1,5},{5... | collective-permute-start | bytes 196616 | tf_op jit(solution)/shard_map/ppermute | solution.py:387
  28.6 4.1 %collective-permute-start.12 = (bf16[256,128]{1,0:T(8,128)(2,1)S(1)}, bf16[256,128]{1,0:T(8,128)(2,1)S(1)}, u32[]{:S(2)}, u32[]{:S(2)}) collective-permute-start(bf16[256,128]{1,0:T(8,128)(2,1)S(1)} %collective-permute-done.11.refs_2_), channel_id=1, source_target_pairs={{0,4},{4,0},{8,12},{12,8},{16,20},{20,16},{24,28},{28,24},{1,5},{5... | collective-permute-start | bytes 196616 | tf_op jit(solution)/shard_map/ppermute | solution.py:387
  30.1 2.7 %collective-permute-start.14 = (bf16[256,128]{1,0:T(8,128)(2,1)S(1)}, bf16[256,128]{1,0:T(8,128)(2,1)S(1)}, u32[]{:S(2)}, u32[]{:S(2)}) collective-permute-start(bf16[256,128]{1,0:T(8,128)(2,1)S(1)} %collective-permute-done.13.refs_4_), channel_id=1, source_target_pairs={{0,4},{4,0},{8,12},{12,8},{16,20},{20,16},{24,28},{28,24},{1,5},{5... | collective-permute-start | bytes 196616 | tf_op jit(solution)/shard_map/ppermute | solution.py:387
  32.7 1.3 %collective-permute-start.16 = (bf16[256,128]{1,0:T(8,128)(2,1)S(1)}, bf16[256,128]{1,0:T(8,128)(2,1)S(1)}, u32[]{:S(2)}, u32[]{:S(2)}) collective-permute-start(bf16[256,128]{1,0:T(8,128)(2,1)S(1)} %collective-permute-done.15.refs_6_), channel_id=1, source_target_pairs={{0,4},{4,0},{8,12},{12,8},{16,20},{20,16},{24,28},{28,24},{1,5},{5... | collective-permute-start | bytes 196616 | tf_op jit(solution)/shard_map/ppermute | solution.py:387
  36.6 6.0 %collective-permute-start.17 = (bf16[48,1024]{1,0:T(8,128)(2,1)S(1)}, bf16[48,1024]{1,0:T(8,128)(2,1)S(1)}, u32[]{:S(2)}, u32[]{:S(2)}) collective-permute-start(bf16[48,1024]{1,0:T(8,128)(2,1)S(1)} %get-tuple-element.32.refs_0_), channel_id=1, source_target_pairs={{0,1},{1,0},{2,3},{3,2},{4,5},{5,4},{6,7},{7,6},{8,9},{9,8},{10,11... | collective-permute-start | bytes 294920 | tf_op jit(solution)/shard_map/ppermute | solution.py:387
  38.0 10.6 %collective-permute-start.18 = (bf16[48,1024]{1,0:T(8,128)(2,1)S(1)}, bf16[48,1024]{1,0:T(8,128)(2,1)S(1)}, u32[]{:S(2)}, u32[]{:S(2)}) collective-permute-start(bf16[48,1024]{1,0:T(8,128)(2,1)S(1)} %get-tuple-element.32.refs_0_), channel_id=1, source_target_pairs={{0,2},{1,3},{2,0},{3,1},{4,6},{5,7},{6,4},{7,5},{8,10},{9,11},{10,... | collective-permute-start | bytes 294920 | tf_op jit(solution)/shard_map/ppermute | solution.py:387
  39.4 9.2 %collective-permute-start.19 = (bf16[48,1024]{1,0:T(8,128)(2,1)S(1)}, bf16[48,1024]{1,0:T(8,128)(2,1)S(1)}, u32[]{:S(2)}, u32[]{:S(2)}) collective-permute-start(bf16[48,1024]{1,0:T(8,128)(2,1)S(1)} %get-tuple-element.32.refs_0_), channel_id=1, source_target_pairs={{0,3},{1,2},{2,1},{3,0},{4,7},{5,6},{6,5},{7,4},{8,11},{9,10},{10,... | collective-permute-start | bytes 294920 | tf_op jit(solution)/shard_map/ppermute | solution.py:387
  51.1 1.3 %collective-permute-start.20 = (bf16[96,256]{1,0:T(8,128)(2,1)S(1)}, bf16[96,256]{1,0:T(8,128)(2,1)S(1)}, u32[]{:S(2)}, u32[]{:S(2)}) collective-permute-start(bf16[96,256]{1,0:T(8,128)(2,1)S(1)} %get-tuple-element.35), channel_id=1, source_target_pairs={{0,4},{4,0},{8,12},{12,8},{16,20},{20,16},{24,28},{28,24},{1,5},{5... | collective-permute-start | bytes 147464 | tf_op jit(solution)/shard_map/ppermute | solution.py:387
  52.4 4.2 %collective-permute-start.21 = (bf16[96,256]{1,0:T(8,128)(2,1)S(1)}, bf16[96,256]{1,0:T(8,128)(2,1)S(1)}, u32[]{:S(2)}, u32[]{:S(2)}) collective-permute-start(bf16[96,256]{1,0:T(8,128)(2,1)S(1)} %add_convert_fusion.3), channel_id=1, source_target_pairs={{0,8},{4,12},{8,0},{12,4},{16,24},{20,28},{24,16},{28,20},{1,9},{5... | collective-permute-start | bytes 147464 | tf_op jit(solution)/shard_map/ppermute | solution.py:387
  54.0 4.4 %collective-permute-start.22 = (bf16[96,256]{1,0:T(8,128)(2,1)S(1)}, bf16[96,256]{1,0:T(8,128)(2,1)S(1)}, u32[]{:S(2)}, u32[]{:S(2)}) collective-permute-start(bf16[96,256]{1,0:T(8,128)(2,1)S(1)} %add_convert_fusion.3), channel_id=1, source_target_pairs={{0,16},{4,20},{8,24},{12,28},{16,0},{20,4},{24,8},{28,12},{1,17},{... | collective-permute-start | bytes 147464 | tf_op jit(solution)/shard_map/ppermute | solution.py:387
  54.2 5.0 %collective-permute-start.23 = (bf16[96,256]{1,0:T(8,128)(2,1)S(1)}, bf16[96,256]{1,0:T(8,128)(2,1)S(1)}, u32[]{:S(2)}, u32[]{:S(2)}) collective-permute-start(bf16[96,256]{1,0:T(8,128)(2,1)S(1)} %add_convert_fusion.3), channel_id=1, source_target_pairs={{0,24},{4,28},{8,16},{12,20},{16,8},{20,12},{24,0},{28,4},{1,25},{... | collective-permute-start | bytes 147464 | tf_op jit(solution)/shard_map/ppermute | solution.py:387
  59.2 4.9 %collective-permute-start.24 = (bf16[96,256]{1,0:T(8,128)(2,1)S(1)}, bf16[96,256]{1,0:T(8,128)(2,1)S(1)}, u32[]{:S(2)}, u32[]{:S(2)}) collective-permute-start(bf16[96,256]{1,0:T(8,128)(2,1)S(1)} %add_convert_fusion.2), channel_id=1, source_target_pairs={{0,1},{1,0},{2,3},{3,2},{4,5},{5,4},{6,7},{7,6},{8,9},{9,8},{10,11... | collective-permute-start | bytes 147464 | tf_op jit(solution)/shard_map/ppermute | solution.py:387
  61.7 5.0 %collective-permute-start.25 = (bf16[96,256]{1,0:T(8,128)(2,1)S(1)}, bf16[96,256]{1,0:T(8,128)(2,1)S(1)}, u32[]{:S(2)}, u32[]{:S(2)}) collective-permute-start(bf16[96,256]{1,0:T(8,128)(2,1)S(1)} %add_convert_fusion.2), channel_id=1, source_target_pairs={{0,2},{1,3},{2,0},{3,1},{4,6},{5,7},{6,4},{7,5},{8,10},{9,11},{10,... | collective-permute-start | bytes 147464 | tf_op jit(solution)/shard_map/ppermute | solution.py:387
  61.7 6.0 %collective-permute-start.26 = (bf16[96,256]{1,0:T(8,128)(2,1)S(1)}, bf16[96,256]{1,0:T(8,128)(2,1)S(1)}, u32[]{:S(2)}, u32[]{:S(2)}) collective-permute-start(bf16[96,256]{1,0:T(8,128)(2,1)S(1)} %add_convert_fusion.2), channel_id=1, source_target_pairs={{0,3},{1,2},{2,1},{3,0},{4,7},{5,6},{6,5},{7,4},{8,11},{9,10},{10,... | collective-permute-start | bytes 147464 | tf_op jit(solution)/shard_map/ppermute | solution.py:387
  67.7 1.3 %collective-permute-start.27 = (bf16[96,256]{1,0:T(8,128)(2,1)S(1)}, bf16[96,256]{1,0:T(8,128)(2,1)S(1)}, u32[]{:S(2)}, u32[]{:S(2)}) collective-permute-start(bf16[96,256]{1,0:T(8,128)(2,1)S(1)} %add_convert_fusion.1.mine), channel_id=1, source_target_pairs={{0,4},{4,0},{8,12},{12,8},{16,20},{20,16},{24,28},{28,24},{1,5},{5... | collective-permute-start | bytes 147464 | tf_op jit(solution)/shard_map/ppermute | solution.py:387

commit v2 on v1

--- a/solution.py
+++ b/solution.py
@@ -297,10 +297,17 @@
     class_both = dot(back_both, column[...])
     packed[pl.ds(features, lines), :] = class_both[:lines] + class_both[lines:]
     twice = jnp.concatenate([class_weight_turned[:lines, :]] * 2, axis=0)
-    hidden_grad = dot(back_both, twice, ((0,), (0,)))
-    pre_grad = hidden_grad * slope[...]
-    packed[pl.ds(0, features), :] = dot(turned[...], pre_grad.astype(bf16))
-    packed[pl.ds(features + lines - 1, 1), :] = jnp.sum(pre_grad, axis=0, keepdims=True)
+    chunk = 2 * nodes
+    weight_grad = jnp.zeros((features, width), f32)
+    bias_grad = jnp.zeros((1, width), f32)
+    for k in range(column.shape[0] // chunk):
+        first, last = k * chunk, (k + 1) * chunk
+        hidden_grad = dot(back_both[:, first:last], twice, ((0,), (0,)))
+        pre_grad = hidden_grad * slope[first:last, :]
+        weight_grad += dot(turned[:, first:last], pre_grad.astype(bf16))
+        bias_grad += jnp.sum(pre_grad, axis=0, keepdims=True)
+    packed[pl.ds(0, features), :] = weight_grad
+    packed[pl.ds(features + lines - 1, 1), :] = bias_grad
     here = (lax.broadcasted_iota(jnp.int32, (8, nodes_row), 1) // nodes == col).astype(f32)
     ours = here.astype(bf16)
     class_sum = dot(ours, high, ((1,), (1,))) + dot(ours, low, ((1,), (1,)))

time: 70.5 us -> 70.5 us (level)
  no operation moved by 1% of the time
where the time goes in v2:
time: 70.5 us; the launch traced here: 70.3 us
  waiting for transfers between devices  28.2 us (40%)
  starting transfers between devices  28 us (40%)
  Pallas kernels  12.4 us (18%)
  between operations  1.51 us (2%)
    ppermute x28, waiting for transfers between devices, swap(): return lax.ppermute(value, axis, [(k, k ^ mask) for k in range(size)])  28.2 us
    ppermute x28, starting transfers between devices, swap(): return lax.ppermute(value, axis, [(k, k ^ mask) for k in range(size)])  28 us
    pallas_call x1, Pallas kernels, hidden_terms(): pl.pallas_call(functools.partial(hidden_kernel, n_row, n_col), out_shape=...  2.6 us
    pallas_call x1, Pallas kernels, gradients(): pl.pallas_call(functools.partial(gradient_kernel, n_col, classes), out_sh...  2.43 us
    pallas_call x1, Pallas kernels, collect(): pl.pallas_call(functools.partial(collect_kernel, group, depth, tile_cols)...  1.9 us
    pallas_call x1, Pallas kernels, first_terms(): pl.pallas_call(functools.partial(first_kernel, n_row, n_col), out_shape=[...  1.85 us
    pallas_call x1, Pallas kernels, slopes(): pl.pallas_call(functools.partial(slope_kernel, n_row), out_shape=[jax.Sha...  1.49 us
  transfers between devices with their start and end apart: 28, of which 18 were waited for; matrix products, arithmetic and copies ran while one was open for 0% of the time, Pallas kernels for 6%

profile of v2, /device:TPU:0, one launch (start us, length us, event | category | flops | bytes accessed | tf_op | source)
XLA Modules:
  0.0 70.3 jit_solution(736880174929109609)
XLA Ops:
  0.6 3.0 %collective-permute-start.1 = (bf16[256,128]{1,0:T(8,128)(2,1)}, bf16[256,128]{1,0:T(8,128)(2,1)S(1)}, u32[]{:S(2)}, u32[]{:S(2)}) collective-permute-start(bf16[256,128]{1,0:T(8,128)(2,1)} %refs_0_.1), channel_id=1, source_target_pairs={{0,8},{4,12},{8,0},{12,4},{16,24},{20,28},{24,16},{28,20},{1,9},{5... | collective-permute-start | bytes 196616 | tf_op jit(solution)/shard_map/ppermute | solution.py:394
  3.7 1.5 %collective-permute-start.3 = (bf16[256,128]{1,0:T(8,128)(2,1)}, bf16[256,128]{1,0:T(8,128)(2,1)S(1)}, u32[]{:S(2)}, u32[]{:S(2)}) collective-permute-start(bf16[256,128]{1,0:T(8,128)(2,1)} %refs_0_.1), channel_id=1, source_target_pairs={{0,16},{4,20},{8,24},{12,28},{16,0},{20,4},{24,8},{28,12},{1,17},{... | collective-permute-start | bytes 196616 | tf_op jit(solution)/shard_map/ppermute | solution.py:394
  5.2 0.0 collective-permute-start.5
  5.9 1.9 %collect.1.total = f32[129,128,128]{2,1,0:T(8,128)S(1)} custom-call(s32[1,1]{1,0:T(1,128)S(6)} %copy.18.count, s32[1,384]{1,0:T(1,128)} %bitcast.19, s32[1,384]{1,0:T(1,128)} %bitcast.20, bf16[384,128,128]{2,1,0:T(8,128)(2,1)} %bitcast.17), custom_call_target="tpu_custom_call" | custom-call | flops 6291456 | bytes 12582912 | tf_op jit(solution)/shard_map/collect/pallas_call | solution.py:96
  7.8 0.0 copy-start.4
  7.9 0.8 %round_block.1.dense = bf16[1024,2048]{1,0:T(8,128)(2,1)S(1)} custom-call(f32[129,128,128]{2,1,0:T(8,128)S(1)} %collect.1.total), custom_call_target="tpu_custom_call" | custom-call | flops 2097152 | bytes 12582912 | tf_op jit(solution)/shard_map/round_block/pallas_call | solution.py:138
  8.7 1.2 %collective-permute-start.2 = (bf16[256,128]{1,0:T(8,128)(2,1)S(1)}, bf16[256,128]{1,0:T(8,128)(2,1)S(1)}, u32[]{:S(2)}, u32[]{:S(2)}) collective-permute-start(bf16[256,128]{1,0:T(8,128)(2,1)S(1)} %collective-permute-done.1.refs_2_), channel_id=1, source_target_pairs={{0,4},{4,0},{8,12},{12,8},{16,20},{20,16},{24,28},{28,24},{1,5},{5... | collective-permute-start | bytes 196616 | tf_op jit(solution)/shard_map/ppermute | solution.py:394
  9.9 0.1 collective-permute-start.4
  10.0 0.6 collective-permute-done.5.refs_6_
  10.6 0.1 pad_add_fusion.ids
  10.6 0.2 collective-permute-done.2.refs_3_
  10.8 0.4 collective-permute-done.4.refs_5_
  11.2 0.6 collective-permute-done.6.refs_7_
  11.8 1.8 %first_terms.1 = (bf16[256,128]{1,0:T(8,128)(2,1)S(1)}, bf16[256,128]{1,0:T(8,128)(2,1)S(1)}, bf16[256,128]{1,0:T(8,128)(2,1)S(1)}, bf16[256,128]{1,0:T(8,128)(2,1)S(1)}) custom-call(s32[2]{0:T(128)S(1)} %pad_add_fusion.ids, bf16[1024,2048]{1,0:T(8,128)(2,1)S(1)} %round_block.1.dense, bf16[256,128]{1,0:T(8,128)(2,1)S(1)} %copy-done, ...), custom_call_target="tpu_custom_call" | custom-call | flops 536870912 | bytes 4194304 | tf_op jit(solution)/shard_map/first_terms/pallas_call | solution.py:164
  13.7 1.6 %collective-permute-start.7 = (bf16[256,128]{1,0:T(8,128)(2,1)S(1)}, bf16[256,128]{1,0:T(8,128)(2,1)S(1)}, u32[]{:S(2)}, u32[]{:S(2)}) collective-permute-start(bf16[256,128]{1,0:T(8,128)(2,1)S(1)} %get-tuple-element.25), channel_id=1, source_target_pairs={{0,1},{1,0},{2,3},{3,2},{4,5},{5,4},{6,7},{7,6},{8,9},{9,8},{10,11... | collective-permute-start | bytes 196616 | tf_op jit(solution)/shard_map/ppermute | solution.py:394
  15.3 2.9 %collective-permute-start.8 = (bf16[256,128]{1,0:T(8,128)(2,1)S(1)}, bf16[256,128]{1,0:T(8,128)(2,1)S(1)}, u32[]{:S(2)}, u32[]{:S(2)}) collective-permute-start(bf16[256,128]{1,0:T(8,128)(2,1)S(1)} %get-tuple-element.26), channel_id=1, source_target_pairs={{0,2},{1,3},{2,0},{3,1},{4,6},{5,7},{6,4},{7,5},{8,10},{9,11},{10,... | collective-permute-start | bytes 196616 | tf_op jit(solution)/shard_map/ppermute | solution.py:394
  18.2 4.2 %collective-permute-done.8 = bf16[256,128]{1,0:T(8,128)(2,1)S(1)} collective-permute-done((bf16[256,128]{1,0:T(8,128)(2,1)S(1)}, bf16[256,128]{1,0:T(8,128)(2,1)S(1)}, u32[]{:S(2)}, u32[]{:S(2)}) %collective-permute-start.8) | collective-permute-done | bytes 65568 | tf_op jit(solution)/shard_map/ppermute | solution.py:394
  22.4 1.9 %collective-permute-done.9 = bf16[256,128]{1,0:T(8,128)(2,1)S(1)} collective-permute-done((bf16[256,128]{1,0:T(8,128)(2,1)S(1)}, bf16[256,128]{1,0:T(8,128)(2,1)S(1)}, u32[]{:S(2)}, u32[]{:S(2)}) %collective-permute-start.9) | collective-permute-done | bytes 65568 | tf_op jit(solution)/shard_map/ppermute | solution.py:394
  24.3 1.5 %collective-permute-start.11 = (bf16[256,128]{1,0:T(8,128)(2,1)S(1)}, bf16[256,128]{1,0:T(8,128)(2,1)S(1)}, u32[]{:S(2)}, u32[]{:S(2)}) collective-permute-start(bf16[256,128]{1,0:T(8,128)(2,1)S(1)} %add_convert_fusion.refs_0_), channel_id=1, source_target_pairs={{0,8},{4,12},{8,0},{12,4},{16,24},{20,28},{24,16},{28,20},{1,9},{5... | collective-permute-start | bytes 196616 | tf_op jit(solution)/shard_map/ppermute | solution.py:394
  25.8 1.7 %collective-permute-start.13 = (bf16[256,128]{1,0:T(8,128)(2,1)S(1)}, bf16[256,128]{1,0:T(8,128)(2,1)S(1)}, u32[]{:S(2)}, u32[]{:S(2)}) collective-permute-start(bf16[256,128]{1,0:T(8,128)(2,1)S(1)} %add_convert_fusion.refs_0_), channel_id=1, source_target_pairs={{0,16},{4,20},{8,24},{12,28},{16,0},{20,4},{24,8},{28,12},{1,17},{... | collective-permute-start | bytes 196616 | tf_op jit(solution)/shard_map/ppermute | solution.py:394
  27.5 0.9 %collective-permute-start.15 = (bf16[256,128]{1,0:T(8,128)(2,1)S(1)}, bf16[256,128]{1,0:T(8,128)(2,1)S(1)}, u32[]{:S(2)}, u32[]{:S(2)}) collective-permute-start(bf16[256,128]{1,0:T(8,128)(2,1)S(1)} %add_convert_fusion.refs_0_), channel_id=1, source_target_pairs={{0,24},{4,28},{8,16},{12,20},{16,8},{20,12},{24,0},{28,4},{1,25},{... | collective-permute-start | bytes 196616 | tf_op jit(solution)/shard_map/ppermute | solution.py:394
  28.5 0.2 collective-permute-done.11.refs_2_
  28.6 0.3 collective-permute-start.12
  29.0 1.1 %collective-permute-done.13.refs_4_ = bf16[256,128]{1,0:T(8,128)(2,1)S(1)} collective-permute-done((bf16[256,128]{1,0:T(8,128)(2,1)S(1)}, bf16[256,128]{1,0:T(8,128)(2,1)S(1)}, u32[]{:S(2)}, u32[]{:S(2)}) %collective-permute-start.13) | collective-permute-done | bytes 65568 | tf_op jit(solution)/shard_map/ppermute | solution.py:394
  30.1 2.6 %collective-permute-done.15.refs_6_ = bf16[256,128]{1,0:T(8,128)(2,1)S(1)} collective-permute-done((bf16[256,128]{1,0:T(8,128)(2,1)S(1)}, bf16[256,128]{1,0:T(8,128)(2,1)S(1)}, u32[]{:S(2)}, u32[]{:S(2)}) %collective-permute-start.15) | collective-permute-done | bytes 65568 | tf_op jit(solution)/shard_map/ppermute | solution.py:394
  32.8 1.2 %collective-permute-done.16.refs_7_ = bf16[256,128]{1,0:T(8,128)(2,1)S(1)} collective-permute-done((bf16[256,128]{1,0:T(8,128)(2,1)S(1)}, bf16[256,128]{1,0:T(8,128)(2,1)S(1)}, u32[]{:S(2)}, u32[]{:S(2)}) %collective-permute-start.16) | collective-permute-done | bytes 65568 | tf_op jit(solution)/shard_map/ppermute | solution.py:394
  34.0 2.6 %hidden_terms.1 = (bf16[256,256]{1,0:T(8,128)(2,1)}, bf16[2048,256]{1,0:T(8,128)(2,1)S(1)}, bf16[48,1024]{1,0:T(8,128)(2,1)S(1)}) custom-call(s32[2]{0:T(128)S(1)} %pad_add_fusion.ids, bf16[1024,2048]{1,0:T(8,128)(2,1)S(1)} %round_block.1.dense, bf16[128,256]{1,0:T(8,128)(2,1)S(1)} %copy-done.1, f32[1,256]{1,0:T(1,128)S(1)} %bitcast.15, ...), custom_call_target="tpu_custom_call" | custom-call | flops 1073741824 | bytes 4194304 | tf_op jit(solution)/shard_map/hidden_terms/pallas_call | solution.py:210
  36.6 1.5 %collective-permute-start.17 = (bf16[48,1024]{1,0:T(8,128)(2,1)S(1)}, bf16[48,1024]{1,0:T(8,128)(2,1)S(1)}, u32[]{:S(2)}, u32[]{:S(2)}) collective-permute-start(bf16[48,1024]{1,0:T(8,128)(2,1)S(1)} %get-tuple-element.32.refs_0_), channel_id=1, source_target_pairs={{0,1},{1,0},{2,3},{3,2},{4,5},{5,4},{6,7},{7,6},{8,9},{9,8},{10,11... | collective-permute-start | bytes 294920 | tf_op jit(solution)/shard_map/ppermute | solution.py:394
  38.0 1.4 %collective-permute-start.18 = (bf16[48,1024]{1,0:T(8,128)(2,1)S(1)}, bf16[48,1024]{1,0:T(8,128)(2,1)S(1)}, u32[]{:S(2)}, u32[]{:S(2)}) collective-permute-start(bf16[48,1024]{1,0:T(8,128)(2,1)S(1)} %get-tuple-element.32.refs_0_), channel_id=1, source_target_pairs={{0,2},{1,3},{2,0},{3,1},{4,6},{5,7},{6,4},{7,5},{8,10},{9,11},{10,... | collective-permute-start | bytes 294920 | tf_op jit(solution)/shard_map/ppermute | solution.py:394
  39.4 1.6 %collective-permute-start.19 = (bf16[48,1024]{1,0:T(8,128)(2,1)S(1)}, bf16[48,1024]{1,0:T(8,128)(2,1)S(1)}, u32[]{:S(2)}, u32[]{:S(2)}) collective-permute-start(bf16[48,1024]{1,0:T(8,128)(2,1)S(1)} %get-tuple-element.32.refs_0_), channel_id=1, source_target_pairs={{0,3},{1,2},{2,1},{3,0},{4,7},{5,6},{6,5},{7,4},{8,11},{9,10},{10,... | collective-permute-start | bytes 294920 | tf_op jit(solution)/shard_map/ppermute | solution.py:394
  41.0 1.5 %slopes.1 = (f32[2048,256]{1,0:T(8,128)S(1)}, bf16[128,2048]{1,0:T(8,128)(2,1)S(1)}) custom-call(s32[2]{0:T(128)S(1)} %pad_add_fusion.ids, bf16[128,256]{1,0:T(8,128)(2,1)S(1)} %copy-done.1, f32[1,256]{1,0:T(1,128)S(1)} %bitcast.16, bf16[256,128]{1,0:T(8,128)(2,1)S(1)} %add_convert_fusion.refs_0_, bf16[256,128]{1,0:T(8,128)(2,1)S(1)} %collective-permute-done.10.refs_1_, ...), custom_call_target="tpu_custom_call" | custom-call | flops 134217728 | bytes 2097152 | tf_op jit(solution)/shard_map/slopes/pallas_call | solution.py:247
  42.5 6.1 %collective-permute-done.18.refs_2_ = bf16[48,1024]{1,0:T(8,128)(2,1)S(1)} collective-permute-done((bf16[48,1024]{1,0:T(8,128)(2,1)S(1)}, bf16[48,1024]{1,0:T(8,128)(2,1)S(1)}, u32[]{:S(2)}, u32[]{:S(2)}) %collective-permute-start.18) | collective-permute-done | bytes 98336 | tf_op jit(solution)/shard_map/ppermute | solution.py:394
  48.6 2.4 %gradients.1 = (f32[47,256]{1,0:T(8,128)}, bf16[96,256]{1,0:T(8,128)(2,1)S(1)}, bf16[96,256]{1,0:T(8,128)(2,1)S(1)}) custom-call(s32[2]{0:T(128)S(1)} %pad_add_fusion.ids, bf16[1024,2048]{1,0:T(8,128)(2,1)S(1)} %round_block.1.dense, bf16[2048,256]{1,0:T(8,128)(2,1)S(1)} %get-tuple-element.29.column, f32[2048,256]{1,0:T(8,128)S(1)} %get-tuple-element.30.slope, ...), custom_call_target="tpu_custom_call" | custom-call | flops 402653184 | bytes 4194304 | tf_op jit(solution)/shard_map/gradients/pallas_call | solution.py:339
  51.1 0.1 collective-permute-start.20
  51.1 1.2 %collective-permute-done.20 = bf16[96,256]{1,0:T(8,128)(2,1)S(1)} collective-permute-done((bf16[96,256]{1,0:T(8,128)(2,1)S(1)}, bf16[96,256]{1,0:T(8,128)(2,1)S(1)}, u32[]{:S(2)}, u32[]{:S(2)}) %collective-permute-start.20) | collective-permute-done | bytes 49184 | tf_op jit(solution)/shard_map/ppermute | solution.py:394
  52.4 1.6 %collective-permute-start.21 = (bf16[96,256]{1,0:T(8,128)(2,1)S(1)}, bf16[96,256]{1,0:T(8,128)(2,1)S(1)}, u32[]{:S(2)}, u32[]{:S(2)}) collective-permute-start(bf16[96,256]{1,0:T(8,128)(2,1)S(1)} %add_convert_fusion.3), channel_id=1, source_target_pairs={{0,8},{4,12},{8,0},{12,4},{16,24},{20,28},{24,16},{28,20},{1,9},{5... | collective-permute-start | bytes 147464 | tf_op jit(solution)/shard_map/ppermute | solution.py:394
  53.9 0.2 collective-permute-start.22
  54.2 1.8 %collective-permute-start.23 = (bf16[96,256]{1,0:T(8,128)(2,1)S(1)}, bf16[96,256]{1,0:T(8,128)(2,1)S(1)}, u32[]{:S(2)}, u32[]{:S(2)}) collective-permute-start(bf16[96,256]{1,0:T(8,128)(2,1)S(1)} %add_convert_fusion.3), channel_id=1, source_target_pairs={{0,24},{4,28},{8,16},{12,20},{16,8},{20,12},{24,0},{28,4},{1,25},{... | collective-permute-start | bytes 147464 | tf_op jit(solution)/shard_map/ppermute | solution.py:394
  55.9 0.6 collective-permute-done.21
  56.5 1.8 %collective-permute-done.22 = bf16[96,256]{1,0:T(8,128)(2,1)S(1)} collective-permute-done((bf16[96,256]{1,0:T(8,128)(2,1)S(1)}, bf16[96,256]{1,0:T(8,128)(2,1)S(1)}, u32[]{:S(2)}, u32[]{:S(2)}) %collective-permute-start.22) | collective-permute-done | bytes 49184 | tf_op jit(solution)/shard_map/ppermute | solution.py:394
  58.4 0.8 %collective-permute-done.23 = bf16[96,256]{1,0:T(8,128)(2,1)S(1)} collective-permute-done((bf16[96,256]{1,0:T(8,128)(2,1)S(1)}, bf16[96,256]{1,0:T(8,128)(2,1)S(1)}, u32[]{:S(2)}, u32[]{:S(2)}) %collective-permute-start.23) | collective-permute-done | bytes 49184 | tf_op jit(solution)/shard_map/ppermute | solution.py:394
  59.2 2.5 %collective-permute-start.24 = (bf16[96,256]{1,0:T(8,128)(2,1)S(1)}, bf16[96,256]{1,0:T(8,128)(2,1)S(1)}, u32[]{:S(2)}, u32[]{:S(2)}) collective-permute-start(bf16[96,256]{1,0:T(8,128)(2,1)S(1)} %add_convert_fusion.2), channel_id=1, source_target_pairs={{0,1},{1,0},{2,3},{3,2},{4,5},{5,4},{6,7},{7,6},{8,9},{9,8},{10,11... | collective-permute-start | bytes 147464 | tf_op jit(solution)/shard_map/ppermute | solution.py:394
  61.7 2.4 %collective-permute-start.26 = (bf16[96,256]{1,0:T(8,128)(2,1)S(1)}, bf16[96,256]{1,0:T(8,128)(2,1)S(1)}, u32[]{:S(2)}, u32[]{:S(2)}) collective-permute-start(bf16[96,256]{1,0:T(8,128)(2,1)S(1)} %add_convert_fusion.2), channel_id=1, source_target_pairs={{0,3},{1,2},{2,1},{3,0},{4,7},{5,6},{6,5},{7,4},{8,11},{9,10},{10,... | collective-permute-start | bytes 147464 | tf_op jit(solution)/shard_map/ppermute | solution.py:394
  64.1 2.6 %collective-permute-done.25 = bf16[96,256]{1,0:T(8,128)(2,1)S(1)} collective-permute-done((bf16[96,256]{1,0:T(8,128)(2,1)S(1)}, bf16[96,256]{1,0:T(8,128)(2,1)S(1)}, u32[]{:S(2)}, u32[]{:S(2)}) %collective-permute-start.25) | collective-permute-done | bytes 49184 | tf_op jit(solution)/shard_map/ppermute | solution.py:394
  66.7 1.0 %collective-permute-done.26 = bf16[96,256]{1,0:T(8,128)(2,1)S(1)} collective-permute-done((bf16[96,256]{1,0:T(8,128)(2,1)S(1)}, bf16[96,256]{1,0:T(8,128)(2,1)S(1)}, u32[]{:S(2)}, u32[]{:S(2)}) %collective-permute-start.26) | collective-permute-done | bytes 49184 | tf_op jit(solution)/shard_map/ppermute | solution.py:394
  67.7 0.1 collective-permute-start.27
  67.8 1.2 %collective-permute-done.27.other = bf16[96,256]{1,0:T(8,128)(2,1)S(1)} collective-permute-done((bf16[96,256]{1,0:T(8,128)(2,1)S(1)}, bf16[96,256]{1,0:T(8,128)(2,1)S(1)}, u32[]{:S(2)}, u32[]{:S(2)}) %collective-permute-start.27) | collective-permute-done | bytes 49184 | tf_op jit(solution)/shard_map/ppermute | solution.py:394
  69.0 1.3 %finish.1 = (f32[1,1]{1,0:T(1,128)}, f32[128,256]{1,0:T(8,128)}, f32[1,256]{1,0:T(1,128)}, f32[47,256]{1,0:T(8,128)}, f32[1,47]{1,0:T(1,128)}) custom-call(s32[2]{0:T(128)S(1)} %pad_add_fusion.ids, bf16[96,256]{1,0:T(8,128)(2,1)S(1)} %add_convert_fusion.1.mine, bf16[96,256]{1,0:T(8,128)(2,1)S(1)} %collective-permute-done.27.other), custom_call_target="tpu_custom_call" | custom-call | tf_op jit(solution)/shard_map/finish/pallas_call | solution.py:375
  (37 shorter events, 0.2 us)
Async XLA Ops:
  0.6 8.1 %collective-permute-start.1 = (bf16[256,128]{1,0:T(8,128)(2,1)}, bf16[256,128]{1,0:T(8,128)(2,1)S(1)}, u32[]{:S(2)}, u32[]{:S(2)}) collective-permute-start(bf16[256,128]{1,0:T(8,128)(2,1)} %refs_0_.1), channel_id=1, source_target_pairs={{0,8},{4,12},{8,0},{12,4},{16,24},{20,28},{24,16},{28,20},{1,9},{5... | collective-permute-start | bytes 196616 | tf_op jit(solution)/shard_map/ppermute | solution.py:394
  3.7 6.2 %collective-permute-start.3 = (bf16[256,128]{1,0:T(8,128)(2,1)}, bf16[256,128]{1,0:T(8,128)(2,1)S(1)}, u32[]{:S(2)}, u32[]{:S(2)}) collective-permute-start(bf16[256,128]{1,0:T(8,128)(2,1)} %refs_0_.1), channel_id=1, source_target_pairs={{0,16},{4,20},{8,24},{12,28},{16,0},{20,4},{24,8},{28,12},{1,17},{... | collective-permute-start | bytes 196616 | tf_op jit(solution)/shard_map/ppermute | solution.py:394
  5.2 5.4 %collective-permute-start.5 = (bf16[256,128]{1,0:T(8,128)(2,1)}, bf16[256,128]{1,0:T(8,128)(2,1)S(1)}, u32[]{:S(2)}, u32[]{:S(2)}) collective-permute-start(bf16[256,128]{1,0:T(8,128)(2,1)} %refs_0_.1), channel_id=1, source_target_pairs={{0,24},{4,28},{8,16},{12,20},{16,8},{20,12},{24,0},{28,4},{1,25},{... | collective-permute-start | bytes 196616 | tf_op jit(solution)/shard_map/ppermute | solution.py:394
  5.2 5.4 %collective-permute-start = (bf16[256,128]{1,0:T(8,128)(2,1)}, bf16[256,128]{1,0:T(8,128)(2,1)S(1)}, u32[]{:S(2)}, u32[]{:S(2)}) collective-permute-start(bf16[256,128]{1,0:T(8,128)(2,1)} %refs_0_.1), channel_id=1, source_target_pairs={{0,4},{4,0},{8,12},{12,8},{16,20},{20,16},{24,28},{28,24},{1,5},{5... | collective-permute-start | bytes 196616 | tf_op jit(solution)/shard_map/ppermute | solution.py:394
  7.8 4.0 %copy-start = (bf16[256,128]{1,0:T(8,128)(2,1)S(1)}, bf16[256,128]{1,0:T(8,128)(2,1)}, u32[]{:S(2)}) copy-start(bf16[256,128]{1,0:T(8,128)(2,1)} %refs_0_.1) | copy-start | bytes 196612
  7.8 24.9 %copy-start.4 = (s32[256]{0:T(256)S(1)}, s32[256]{0:T(256)}, u32[]{:S(2)}) copy-start(s32[256]{0:T(256)} %param.16) | copy-start | bytes 3076
  7.8 24.9 %copy-start.5 = (s32[256]{0:T(256)S(1)}, s32[256]{0:T(256)}, u32[]{:S(2)}) copy-start(s32[256]{0:T(256)} %param.17) | copy-start | bytes 3076
  7.8 24.9 %copy-start.3 = (bf16[256,47]{0,1:T(8,128)(2,1)S(1)}, bf16[256,47]{0,1:T(8,128)(2,1)}, u32[]{:S(2)}) copy-start(bf16[256,47]{0,1:T(8,128)(2,1)} %param.20) | copy-start | bytes 72196
  7.8 26.1 %copy-start.1 = (bf16[128,256]{1,0:T(8,128)(2,1)S(1)}, bf16[128,256]{1,0:T(8,128)(2,1)}, u32[]{:S(2)}) copy-start(bf16[128,256]{1,0:T(8,128)(2,1)} %weight.3) | copy-start | bytes 196612
  7.8 26.1 %copy-start.2 = (f32[256]{0:T(256)S(1)}, f32[256]{0:T(256)}, u32[]{:S(2)}) copy-start(f32[256]{0:T(256)} %param.19) | copy-start | bytes 3076
  7.8 33.2 %copy-start.6 = (f32[47]{0:T(128)S(1)}, f32[47]{0:T(128)}, u32[]{:S(2)}) copy-start(f32[47]{0:T(128)} %param.21) | copy-start | bytes 568
  8.7 2.1 %collective-permute-start.2 = (bf16[256,128]{1,0:T(8,128)(2,1)S(1)}, bf16[256,128]{1,0:T(8,128)(2,1)S(1)}, u32[]{:S(2)}, u32[]{:S(2)}) collective-permute-start(bf16[256,128]{1,0:T(8,128)(2,1)S(1)} %collective-permute-done.1.refs_2_), channel_id=1, source_target_pairs={{0,4},{4,0},{8,12},{12,8},{16,20},{20,16},{24,28},{28,24},{1,5},{5... | collective-permute-start | bytes 196616 | tf_op jit(solution)/shard_map/ppermute | solution.py:394
  9.9 1.3 %collective-permute-start.4 = (bf16[256,128]{1,0:T(8,128)(2,1)S(1)}, bf16[256,128]{1,0:T(8,128)(2,1)S(1)}, u32[]{:S(2)}, u32[]{:S(2)}) collective-permute-start(bf16[256,128]{1,0:T(8,128)(2,1)S(1)} %collective-permute-done.3.refs_4_), channel_id=1, source_target_pairs={{0,4},{4,0},{8,12},{12,8},{16,20},{20,16},{24,28},{28,24},{1,5},{5... | collective-permute-start | bytes 196616 | tf_op jit(solution)/shard_map/ppermute | solution.py:394
  10.6 1.3 %collective-permute-start.6 = (bf16[256,128]{1,0:T(8,128)(2,1)S(1)}, bf16[256,128]{1,0:T(8,128)(2,1)S(1)}, u32[]{:S(2)}, u32[]{:S(2)}) collective-permute-start(bf16[256,128]{1,0:T(8,128)(2,1)S(1)} %collective-permute-done.5.refs_6_), channel_id=1, source_target_pairs={{0,4},{4,0},{8,12},{12,8},{16,20},{20,16},{24,28},{28,24},{1,5},{5... | collective-permute-start | bytes 196616 | tf_op jit(solution)/shard_map/ppermute | solution.py:394
  13.7 4.5 %collective-permute-start.7 = (bf16[256,128]{1,0:T(8,128)(2,1)S(1)}, bf16[256,128]{1,0:T(8,128)(2,1)S(1)}, u32[]{:S(2)}, u32[]{:S(2)}) collective-permute-start(bf16[256,128]{1,0:T(8,128)(2,1)S(1)} %get-tuple-element.25), channel_id=1, source_target_pairs={{0,1},{1,0},{2,3},{3,2},{4,5},{5,4},{6,7},{7,6},{8,9},{9,8},{10,11... | collective-permute-start | bytes 196616 | tf_op jit(solution)/shard_map/ppermute | solution.py:394
  15.3 7.1 %collective-permute-start.8 = (bf16[256,128]{1,0:T(8,128)(2,1)S(1)}, bf16[256,128]{1,0:T(8,128)(2,1)S(1)}, u32[]{:S(2)}, u32[]{:S(2)}) collective-permute-start(bf16[256,128]{1,0:T(8,128)(2,1)S(1)} %get-tuple-element.26), channel_id=1, source_target_pairs={{0,2},{1,3},{2,0},{3,1},{4,6},{5,7},{6,4},{7,5},{8,10},{9,11},{10,... | collective-permute-start | bytes 196616 | tf_op jit(solution)/shard_map/ppermute | solution.py:394
  18.2 6.1 %collective-permute-start.9 = (bf16[256,128]{1,0:T(8,128)(2,1)S(1)}, bf16[256,128]{1,0:T(8,128)(2,1)S(1)}, u32[]{:S(2)}, u32[]{:S(2)}) collective-permute-start(bf16[256,128]{1,0:T(8,128)(2,1)S(1)} %get-tuple-element.27), channel_id=1, source_target_pairs={{0,3},{1,2},{2,1},{3,0},{4,7},{5,6},{6,5},{7,4},{8,11},{9,10},{10,... | collective-permute-start | bytes 196616 | tf_op jit(solution)/shard_map/ppermute | solution.py:394
  24.3 4.3 %collective-permute-start.11 = (bf16[256,128]{1,0:T(8,128)(2,1)S(1)}, bf16[256,128]{1,0:T(8,128)(2,1)S(1)}, u32[]{:S(2)}, u32[]{:S(2)}) collective-permute-start(bf16[256,128]{1,0:T(8,128)(2,1)S(1)} %add_convert_fusion.refs_0_), channel_id=1, source_target_pairs={{0,8},{4,12},{8,0},{12,4},{16,24},{20,28},{24,16},{28,20},{1,9},{5... | collective-permute-start | bytes 196616 | tf_op jit(solution)/shard_map/ppermute | solution.py:394
  25.8 4.3 %collective-permute-start.13 = (bf16[256,128]{1,0:T(8,128)(2,1)S(1)}, bf16[256,128]{1,0:T(8,128)(2,1)S(1)}, u32[]{:S(2)}, u32[]{:S(2)}) collective-permute-start(bf16[256,128]{1,0:T(8,128)(2,1)S(1)} %add_convert_fusion.refs_0_), channel_id=1, source_target_pairs={{0,16},{4,20},{8,24},{12,28},{16,0},{20,4},{24,8},{28,12},{1,17},{... | collective-permute-start | bytes 196616 | tf_op jit(solution)/shard_map/ppermute | solution.py:394
  27.5 5.2 %collective-permute-start.15 = (bf16[256,128]{1,0:T(8,128)(2,1)S(1)}, bf16[256,128]{1,0:T(8,128)(2,1)S(1)}, u32[]{:S(2)}, u32[]{:S(2)}) collective-permute-start(bf16[256,128]{1,0:T(8,128)(2,1)S(1)} %add_convert_fusion.refs_0_), channel_id=1, source_target_pairs={{0,24},{4,28},{8,16},{12,20},{16,8},{20,12},{24,0},{28,4},{1,25},{... | collective-permute-start | bytes 196616 | tf_op jit(solution)/shard_map/ppermute | solution.py:394
  28.5 4.3 %collective-permute-start.10 = (bf16[256,128]{1,0:T(8,128)(2,1)S(1)}, bf16[256,128]{1,0:T(8,128)(2,1)S(1)}, u32[]{:S(2)}, u32[]{:S(2)}) collective-permute-start(bf16[256,128]{1,0:T(8,128)(2,1)S(1)} %add_convert_fusion.refs_0_), channel_id=1, source_target_pairs={{0,4},{4,0},{8,12},{12,8},{16,20},{20,16},{24,28},{28,24},{1,5},{5... | collective-permute-start | bytes 196616 | tf_op jit(solution)/shard_map/ppermute | solution.py:394
  28.6 4.1 %collective-permute-start.12 = (bf16[256,128]{1,0:T(8,128)(2,1)S(1)}, bf16[256,128]{1,0:T(8,128)(2,1)S(1)}, u32[]{:S(2)}, u32[]{:S(2)}) collective-permute-start(bf16[256,128]{1,0:T(8,128)(2,1)S(1)} %collective-permute-done.11.refs_2_), channel_id=1, source_target_pairs={{0,4},{4,0},{8,12},{12,8},{16,20},{20,16},{24,28},{28,24},{1,5},{5... | collective-permute-start | bytes 196616 | tf_op jit(solution)/shard_map/ppermute | solution.py:394
  30.1 2.7 %collective-permute-start.14 = (bf16[256,128]{1,0:T(8,128)(2,1)S(1)}, bf16[256,128]{1,0:T(8,128)(2,1)S(1)}, u32[]{:S(2)}, u32[]{:S(2)}) collective-permute-start(bf16[256,128]{1,0:T(8,128)(2,1)S(1)} %collective-permute-done.13.refs_4_), channel_id=1, source_target_pairs={{0,4},{4,0},{8,12},{12,8},{16,20},{20,16},{24,28},{28,24},{1,5},{5... | collective-permute-start | bytes 196616 | tf_op jit(solution)/shard_map/ppermute | solution.py:394
  32.7 1.3 %collective-permute-start.16 = (bf16[256,128]{1,0:T(8,128)(2,1)S(1)}, bf16[256,128]{1,0:T(8,128)(2,1)S(1)}, u32[]{:S(2)}, u32[]{:S(2)}) collective-permute-start(bf16[256,128]{1,0:T(8,128)(2,1)S(1)} %collective-permute-done.15.refs_6_), channel_id=1, source_target_pairs={{0,4},{4,0},{8,12},{12,8},{16,20},{20,16},{24,28},{28,24},{1,5},{5... | collective-permute-start | bytes 196616 | tf_op jit(solution)/shard_map/ppermute | solution.py:394
  36.6 6.0 %collective-permute-start.17 = (bf16[48,1024]{1,0:T(8,128)(2,1)S(1)}, bf16[48,1024]{1,0:T(8,128)(2,1)S(1)}, u32[]{:S(2)}, u32[]{:S(2)}) collective-permute-start(bf16[48,1024]{1,0:T(8,128)(2,1)S(1)} %get-tuple-element.32.refs_0_), channel_id=1, source_target_pairs={{0,1},{1,0},{2,3},{3,2},{4,5},{5,4},{6,7},{7,6},{8,9},{9,8},{10,11... | collective-permute-start | bytes 294920 | tf_op jit(solution)/shard_map/ppermute | solution.py:394
  38.0 10.6 %collective-permute-start.18 = (bf16[48,1024]{1,0:T(8,128)(2,1)S(1)}, bf16[48,1024]{1,0:T(8,128)(2,1)S(1)}, u32[]{:S(2)}, u32[]{:S(2)}) collective-permute-start(bf16[48,1024]{1,0:T(8,128)(2,1)S(1)} %get-tuple-element.32.refs_0_), channel_id=1, source_target_pairs={{0,2},{1,3},{2,0},{3,1},{4,6},{5,7},{6,4},{7,5},{8,10},{9,11},{10,... | collective-permute-start | bytes 294920 | tf_op jit(solution)/shard_map/ppermute | solution.py:394
  39.4 9.2 %collective-permute-start.19 = (bf16[48,1024]{1,0:T(8,128)(2,1)S(1)}, bf16[48,1024]{1,0:T(8,128)(2,1)S(1)}, u32[]{:S(2)}, u32[]{:S(2)}) collective-permute-start(bf16[48,1024]{1,0:T(8,128)(2,1)S(1)} %get-tuple-element.32.refs_0_), channel_id=1, source_target_pairs={{0,3},{1,2},{2,1},{3,0},{4,7},{5,6},{6,5},{7,4},{8,11},{9,10},{10,... | collective-permute-start | bytes 294920 | tf_op jit(solution)/shard_map/ppermute | solution.py:394
  51.1 1.3 %collective-permute-start.20 = (bf16[96,256]{1,0:T(8,128)(2,1)S(1)}, bf16[96,256]{1,0:T(8,128)(2,1)S(1)}, u32[]{:S(2)}, u32[]{:S(2)}) collective-permute-start(bf16[96,256]{1,0:T(8,128)(2,1)S(1)} %get-tuple-element.35), channel_id=1, source_target_pairs={{0,4},{4,0},{8,12},{12,8},{16,20},{20,16},{24,28},{28,24},{1,5},{5... | collective-permute-start | bytes 147464 | tf_op jit(solution)/shard_map/ppermute | solution.py:394
  52.4 4.2 %collective-permute-start.21 = (bf16[96,256]{1,0:T(8,128)(2,1)S(1)}, bf16[96,256]{1,0:T(8,128)(2,1)S(1)}, u32[]{:S(2)}, u32[]{:S(2)}) collective-permute-start(bf16[96,256]{1,0:T(8,128)(2,1)S(1)} %add_convert_fusion.3), channel_id=1, source_target_pairs={{0,8},{4,12},{8,0},{12,4},{16,24},{20,28},{24,16},{28,20},{1,9},{5... | collective-permute-start | bytes 147464 | tf_op jit(solution)/shard_map/ppermute | solution.py:394
  53.9 4.4 %collective-permute-start.22 = (bf16[96,256]{1,0:T(8,128)(2,1)S(1)}, bf16[96,256]{1,0:T(8,128)(2,1)S(1)}, u32[]{:S(2)}, u32[]{:S(2)}) collective-permute-start(bf16[96,256]{1,0:T(8,128)(2,1)S(1)} %add_convert_fusion.3), channel_id=1, source_target_pairs={{0,16},{4,20},{8,24},{12,28},{16,0},{20,4},{24,8},{28,12},{1,17},{... | collective-permute-start | bytes 147464 | tf_op jit(solution)/shard_map/ppermute | solution.py:394
  54.2 5.0 %collective-permute-start.23 = (bf16[96,256]{1,0:T(8,128)(2,1)S(1)}, bf16[96,256]{1,0:T(8,128)(2,1)S(1)}, u32[]{:S(2)}, u32[]{:S(2)}) collective-permute-start(bf16[96,256]{1,0:T(8,128)(2,1)S(1)} %add_convert_fusion.3), channel_id=1, source_target_pairs={{0,24},{4,28},{8,16},{12,20},{16,8},{20,12},{24,0},{28,4},{1,25},{... | collective-permute-start | bytes 147464 | tf_op jit(solution)/shard_map/ppermute | solution.py:394
  59.2 5.0 %collective-permute-start.24 = (bf16[96,256]{1,0:T(8,128)(2,1)S(1)}, bf16[96,256]{1,0:T(8,128)(2,1)S(1)}, u32[]{:S(2)}, u32[]{:S(2)}) collective-permute-start(bf16[96,256]{1,0:T(8,128)(2,1)S(1)} %add_convert_fusion.2), channel_id=1, source_target_pairs={{0,1},{1,0},{2,3},{3,2},{4,5},{5,4},{6,7},{7,6},{8,9},{9,8},{10,11... | collective-permute-start | bytes 147464 | tf_op jit(solution)/shard_map/ppermute | solution.py:394
  61.7 5.0 %collective-permute-start.25 = (bf16[96,256]{1,0:T(8,128)(2,1)S(1)}, bf16[96,256]{1,0:T(8,128)(2,1)S(1)}, u32[]{:S(2)}, u32[]{:S(2)}) collective-permute-start(bf16[96,256]{1,0:T(8,128)(2,1)S(1)} %add_convert_fusion.2), channel_id=1, source_target_pairs={{0,2},{1,3},{2,0},{3,1},{4,6},{5,7},{6,4},{7,5},{8,10},{9,11},{10,... | collective-permute-start | bytes 147464 | tf_op jit(solution)/shard_map/ppermute | solution.py:394
  61.7 6.0 %collective-permute-start.26 = (bf16[96,256]{1,0:T(8,128)(2,1)S(1)}, bf16[96,256]{1,0:T(8,128)(2,1)S(1)}, u32[]{:S(2)}, u32[]{:S(2)}) collective-permute-start(bf16[96,256]{1,0:T(8,128)(2,1)S(1)} %add_convert_fusion.2), channel_id=1, source_target_pairs={{0,3},{1,2},{2,1},{3,0},{4,7},{5,6},{6,5},{7,4},{8,11},{9,10},{10,... | collective-permute-start | bytes 147464 | tf_op jit(solution)/shard_map/ppermute | solution.py:394
  67.7 1.3 %collective-permute-start.27 = (bf16[96,256]{1,0:T(8,128)(2,1)S(1)}, bf16[96,256]{1,0:T(8,128)(2,1)S(1)}, u32[]{:S(2)}, u32[]{:S(2)}) collective-permute-start(bf16[96,256]{1,0:T(8,128)(2,1)S(1)} %add_convert_fusion.1.mine), channel_id=1, source_target_pairs={{0,4},{4,0},{8,12},{12,8},{16,20},{20,16},{24,28},{28,24},{1,5},{5... | collective-permute-start | bytes 147464 | tf_op jit(solution)/shard_map/ppermute | solution.py:394
